TPU v7x, 128 devices: a whole 4x4x4 slice. The times are simulated.
128 devices in a mesh: wide: 16 (over x, z), narrow: 8 (over y, core).
Axes of the slice: x: 4, y: 4, z: 4, core: 2. Of those that a mesh axis runs over, the one named last changes fastest.
Arguments:
- user_table: bfloat16 [65536, 256], P('wide'), may hold values from -3 to 3
- item_table: bfloat16 [32768, 256], P('wide'), may hold values from -3 to 3
- week_table: bfloat16 [1024, 256], P('wide'), may hold values from -3 to 3
- profile: bfloat16 [65536, 4096], P('wide', 'narrow'), may hold values from -6 to 6
- feature_table: bfloat16 [4096, 256], P('narrow'), may hold values from -0.375 to 0.375
- user_req: int32 [128, 16, 32], P(('wide', 'narrow')), may hold values from 0 to 4095
- item_req: int32 [128, 16, 32], P(('wide', 'narrow')), may hold values from 0 to 2047
- week_req: int32 [128, 16, 4], P(('wide', 'narrow')), may hold values from 0 to 63
- user_counts: int32 [128, 16], P(('wide', 'narrow')), may hold values from 1 to 32, 256 in all within a row
- item_counts: int32 [128, 16], P(('wide', 'narrow')), may hold values from 1 to 32, 256 in all within a row
- week_counts: int32 [128, 16], P(('wide', 'narrow')), may hold values from 1 to 4, 28 in all within a row
- pos_cells: int32 [128, 4096], P(('wide', 'narrow')), may hold values from 0 to 1835007
Outputs:
- grad_users: float32 [65536, 256], P(('wide', 'narrow'))
- grad_items: float32 [32768, 256], P(('wide', 'narrow'))
- grad_weeks: float32 [1024, 256], P(('wide', 'narrow'))
- grad_features: float32 [4096, 256], P('narrow')
Inputs may be any that keep to these rules, and one draw needn't show every extreme that they name: `user_req`: only the first user_counts[d, o] slots of owner o are read; the rest hold arbitrary row numbers. Rows may repeat. `item_req`: only the first item_counts[d, o] slots of owner o are read. `week_req`: only the first week_counts[d, o] slots of owner o are read. `user_counts`: each block's counts sum to 256; every block has an owner with exactly 32. `item_counts`: each block's counts sum to 256; every block has an owner with exactly 32. `week_counts`: each block's counts sum to 28; every block has an owner with exactly 4. `pos_cells`: cells may repeat.
All inputs are finite; a program needn't handle non-finite values.
Results may differ from a plain program's by a relative error of at most 0.0015.
Values may be sent and summed in bfloat16 or wider, within the bound.
A program may use at most 128 MiB of HBM per device.

v0:
```python
import jax
import jax.numpy as jnp
from jax import lax
from jax.sharding import PartitionSpec as P

RANK = 256
BU = 256
BI = 256
BW = 28
CAPU = 32
CAPI = 32
CAPW = 4


def compact_index(counts, cap, total):
    ends = jnp.cumsum(counts)
    starts = ends - counts
    place = jnp.arange(total, dtype=jnp.int32)
    owner = jnp.sum((ends[None, :] <= place[:, None]).astype(jnp.int32), axis=1)
    onehot = (owner[:, None] == jnp.arange(counts.shape[0], dtype=jnp.int32)[None, :]).astype(
        jnp.int32
    )
    first = jnp.sum(onehot * starts[None, :], axis=1)
    return owner * cap + place - first


def block_grads(user_rows, item_rows, week_rows, pos):
    nweek, nuser, nitem = (week_rows.shape[0], user_rows.shape[0], item_rows.shape[0])
    user_f = user_rows.astype(jnp.float32)
    week_f = week_rows.astype(jnp.float32)
    mixed = (user_f[None] * week_f[:, None]).astype(jnp.bfloat16)
    model = jnp.einsum("kir,jr->kij", mixed, item_rows, preferred_element_type=jnp.float32)
    cells = nweek * nuser * nitem
    cpos = jnp.zeros((cells,), jnp.float32).at[pos].set(1.0).reshape(nweek, nuser, nitem)
    resid = (jax.nn.sigmoid(model) - cpos).astype(jnp.bfloat16)
    partial_value = jnp.einsum("kij,jr->kir", resid, item_rows, preferred_element_type=jnp.float32)
    grad_u = jnp.sum(partial_value * week_f[:, None, :], axis=0)
    grad_w = jnp.sum(partial_value * user_f[None], axis=1)
    grad_v = jnp.einsum("kij,kir->jr", resid, mixed, preferred_element_type=jnp.float32)
    return (grad_u, grad_v, grad_w)


def into_slots(grads, flat, owners, cap):
    slots = jnp.zeros((owners * cap, grads.shape[1]), jnp.float32).at[flat].set(grads)
    return slots.reshape(owners, cap, grads.shape[1])


def local(
    user_table,
    item_table,
    week_table,
    profile,
    feature_table,
    user_req,
    item_req,
    week_req,
    user_counts,
    item_counts,
    week_counts,
    pos_cells,
):
    owners = lax.axis_size("wide")
    shares = lax.axis_size("narrow")
    user_need, item_need, week_need = (user_req[0], item_req[0], week_req[0])
    user_flat = compact_index(user_counts[0], CAPU, BU)
    item_flat = compact_index(item_counts[0], CAPI, BI)
    week_flat = compact_index(week_counts[0], CAPW, BW)
    own_users, own_items, own_weeks = (
        user_table.shape[0],
        item_table.shape[0],
        week_table.shape[0],
    )
    got_u, got_v, got_w = (
        lax.all_to_all(user_need, "wide", split_axis=0, concat_axis=0, tiled=True),
        lax.all_to_all(item_need, "wide", split_axis=0, concat_axis=0, tiled=True),
        lax.all_to_all(week_need, "wide", split_axis=0, concat_axis=0, tiled=True),
    )
    back_u, back_v, back_w = (
        lax.all_to_all(user_table[got_u], "wide", split_axis=0, concat_axis=0, tiled=True),
        lax.all_to_all(item_table[got_v], "wide", split_axis=0, concat_axis=0, tiled=True),
        lax.all_to_all(week_table[got_w], "wide", split_axis=0, concat_axis=0, tiled=True),
    )
    week_rows = back_w.reshape(-1, RANK)[week_flat]
    user_rows = back_u.reshape(-1, RANK)[user_flat]
    item_rows = back_v.reshape(-1, RANK)[item_flat]
    grad_u, grad_v, grad_w = block_grads(user_rows, item_rows, week_rows, pos_cells[0])
    slots_u = into_slots(grad_u, user_flat, owners, CAPU)
    slots_v = into_slots(grad_v, item_flat, owners, CAPI)
    slots_w = into_slots(grad_w, week_flat, owners, CAPW)
    ret_u, ret_v, ret_w = (
        lax.all_to_all(slots_u, "wide", split_axis=0, concat_axis=0, tiled=True),
        lax.all_to_all(slots_v, "wide", split_axis=0, concat_axis=0, tiled=True),
        lax.all_to_all(slots_w, "wide", split_axis=0, concat_axis=0, tiled=True),
    )
    dense_w = (
        jnp.zeros((own_weeks, RANK), jnp.float32).at[got_w.reshape(-1)].add(ret_w.reshape(-1, RANK))
    )
    dense_u = (
        jnp.zeros((own_users, RANK), jnp.float32).at[got_u.reshape(-1)].add(ret_u.reshape(-1, RANK))
    )
    dense_v = (
        jnp.zeros((own_items, RANK), jnp.float32).at[got_v.reshape(-1)].add(ret_v.reshape(-1, RANK))
    )
    model = lax.dot_general(
        user_table, feature_table, (((1,), (1,)), ((), ())), preferred_element_type=jnp.float32
    )
    resid = (model - profile.astype(jnp.float32)).astype(jnp.bfloat16)
    dense_u = dense_u + 0.0625 * jnp.dot(resid, feature_table, preferred_element_type=jnp.float32)
    feat_terms = 0.0625 * lax.dot_general(
        resid, user_table, (((0,), (0,)), ((), ())), preferred_element_type=jnp.float32
    )
    grad_features = lax.psum(feat_terms, "wide")
    total_u, total_v, total_w = lax.psum((dense_u, dense_v, dense_w), "narrow")
    place = lax.axis_index("narrow")
    grad_users = lax.dynamic_slice_in_dim(
        total_u, place * (own_users // shares), own_users // shares, 0
    )
    grad_items = lax.dynamic_slice_in_dim(
        total_v, place * (own_items // shares), own_items // shares, 0
    )
    grad_weeks = lax.dynamic_slice_in_dim(
        total_w, place * (own_weeks // shares), own_weeks // shares, 0
    )
    return (grad_users, grad_items, grad_weeks, grad_features)


def solution(mesh):
    return jax.shard_map(
        local,
        mesh=mesh,
        in_specs=(
            P("wide", None),
            P("wide", None),
            P("wide", None),
            P("wide", "narrow"),
            P("narrow", None),
            P(("wide", "narrow"), None, None),
            P(("wide", "narrow"), None, None),
            P(("wide", "narrow"), None, None),
            P(("wide", "narrow"), None),
            P(("wide", "narrow"), None),
            P(("wide", "narrow"), None),
            P(("wide", "narrow"), None),
        ),
        out_specs=(
            P(("wide", "narrow"), None),
            P(("wide", "narrow"), None),
            P(("wide", "narrow"), None),
            P("narrow", None),
        ),
        check_vma=False,
    )
```

profile of v0, /device:TPU:1, one launch (start us, length us, event | category | flops | bytes accessed | tf_op | source)
XLA Modules:
  0.0 353.6 jit_solution(6961960536164734551)
XLA Ops:
  8.7 8.4 %all-to-all-start.2 = ((s32[16,1,4]{2,1,0:T(1,128)}), s32[16,1,4]{2,1,0:T(1,128)S(1)}, u32[]{:S(2)}, u32[]{:S(2)}) async-start(s32[16,1,4]{2,1,0:T(1,128)} %copy.36), calls=%async_computation.2 | async-start | bytes 16384 | tf_op jit(solution)/shard_map/all_to_all | solution.py:76
  23.5 6.3 %all-to-all-start = ((s32[16,1,32]{2,1,0:T(1,128)}), s32[16,1,32]{2,1,0:T(1,128)S(1)}, u32[]{:S(2)}, u32[]{:S(2)}) async-start(s32[16,1,32]{2,1,0:T(1,128)} %bitcast.92), calls=%async_computation | async-start | bytes 16384 | tf_op jit(solution)/shard_map/all_to_all | solution.py:74
  32.1 4.0 %all-to-all-done = s32[16,1,32]{2,1,0:T(1,128)S(1)} async-done(((s32[16,1,32]{2,1,0:T(1,128)}), s32[16,1,32]{2,1,0:T(1,128)S(1)}, u32[]{:S(2)}, u32[]{:S(2)}) %all-to-all-start) | async-done | bytes 2080 | tf_op jit(solution)/shard_map/all_to_all | solution.py:74
  36.1 3.5 all-to-all-start.4
  39.7 6.2 %all-to-all-done.4 = s32[16,1,32]{2,1,0:T(1,128)S(1)} async-done(((s32[16,1,32]{2,1,0:T(1,128)}), s32[16,1,32]{2,1,0:T(1,128)S(1)}, u32[]{:S(2)}, u32[]{:S(2)}) %all-to-all-start.4) | async-done | bytes 2080 | tf_op jit(solution)/shard_map/all_to_all | solution.py:75
  45.8 3.5 all-to-all-start.3
  52.0 3.8 %all-to-all-done.3 = bf16[16,4,256]{2,1,0:T(4,128)(2,1)S(1)} async-done(((bf16[16,4,256]{2,1,0:T(4,128)(2,1)}), bf16[16,4,256]{2,1,0:T(4,128)(2,1)S(1)}, u32[]{:S(2)}, u32[]{:S(2)}) %all-to-all-start.3) | async-done | bytes 32800 | tf_op jit(solution)/shard_map/all_to_all | solution.py:81
  55.8 3.5 all-to-all-start.1
  62.0 4.6 %all-to-all-done.1 = bf16[16,32,256]{2,1,0:T(8,128)(2,1)S(1)} async-done(((bf16[16,32,256]{2,1,0:T(8,128)(2,1)}), bf16[16,32,256]{2,1,0:T(8,128)(2,1)S(1)}, u32[]{:S(2)}, u32[]{:S(2)}) %all-to-all-start.1) | async-done | bytes 262176 | tf_op jit(solution)/shard_map/all_to_all | solution.py:79
  66.6 3.5 all-to-all-start.5
  70.2 18.9 %scatter_custom_fusion = f32[1835008]{0:T(1024)} fusion(s32[4096]{0:T(1024)S(1)} %bitcast.90, f32[4096]{0:T(1024)S(1)} %broadcast.222, f32[]{:T(128)} %constant.17.clone.1), kind=kCustom, calls=%fused_computation.21 | custom fusion | bytes 7340036 | tf_op jit(solution)/shard_map/scatter | solution.py:34
  89.1 9.4 %reshape.400 = f32[28,256,256]{2,1,0:T(8,128)} reshape(f32[1835008]{0:T(1024)} %scatter_custom_fusion) | data formatting | bytes 14680064 | tf_op jit(solution)/shard_map/reshape | solution.py:34
  101.5 4.5 %subtract_convert_fusion.1 = bf16[28,256,256]{2,1,0:T(8,128)(2,1)S(1)} fusion(f32[28,256,256]{2,1,0:T(8,128)} %reshape.400, f32[28,256]{1,0:T(8,128)S(1)} %convert_element_type.43, f32[256,256]{1,0:T(8,128)S(1)} %convert_element_type.41, bf16[256,256]{1,0:T(8,128)(2,1)S(1)} %gather_fusion.5), kind=kOutput, calls=%fused_computation.16 | convolution fusion | flops 952369152 | bytes 11431936 | tf_op jit(solution)/shard_map/kir,jr->kij/dot_general | solution.py:32
  109.2 6.6 %all-to-all-start.8 = ((f32[16,4,256]{2,1,0:T(4,128)}), f32[16,4,256]{2,1,0:T(4,128)S(1)}, u32[]{:S(2)}, u32[]{:S(2)}) async-start(f32[16,4,256]{2,1,0:T(4,128)} %reshape.407), calls=%async_computation.8 | async-start | bytes 131072 | tf_op jit(solution)/shard_map/all_to_all | solution.py:93
  115.8 3.9 %fusion.8 = f32[256,256]{1,0:T(8,128)} fusion(bf16[28,256,256]{2,1,0:T(8,128)(2,1)} %copy-done.4, f32[28,256]{1,0:T(8,128)S(1)} %convert_element_type.43, f32[256,256]{1,0:T(8,128)S(1)} %convert_element_type.41), kind=kOutput, calls=%fused_computation.28 | convolution fusion | flops 943194112 | bytes 4222976 | tf_op jit(solution)/shard_map/kij,kir->jr/dot_general | solution.py:39
  122.3 6.6 %all-to-all-start.7 = ((f32[16,32,256]{2,1,0:T(8,128)}), f32[16,32,256]{2,1,0:T(8,128)S(1)}, u32[]{:S(2)}, u32[]{:S(2)}) async-start(f32[16,32,256]{2,1,0:T(8,128)} %bitcast.33), calls=%async_computation.7 | async-start | bytes 1048576 | tf_op jit(solution)/shard_map/all_to_all | solution.py:92
  129.0 3.5 subtract_convert_fusion
  134.4 3.2 convolution_multiply_fusion
  141.1 6.7 %all-to-all-start.6 = ((f32[16,32,256]{2,1,0:T(8,128)}), f32[16,32,256]{2,1,0:T(8,128)S(1)}, u32[]{:S(2)}, u32[]{:S(2)}) async-start(f32[16,32,256]{2,1,0:T(8,128)} %bitcast.29), calls=%async_computation.6 | async-start | bytes 1048576 | tf_op jit(solution)/shard_map/all_to_all | solution.py:91
  150.9 4.8 %scatter_custom_fusion.4 = f32[2048,256]{1,0:T(8,128)} fusion(s32[512]{0:T(512)S(1)} %bitcast.103, f32[512,256]{1,0:T(8,128)S(1)} %bitcast.87, f32[]{:T(128)} %constant.17.clone.1), kind=kCustom, calls=%fused_computation.29 | custom fusion | flops 131072 | bytes 2097156 | tf_op jit(solution)/shard_map/scatter-add | solution.py:102
  156.7 7.2 %scatter_fusion = f32[4096,256]{1,0:T(8,128)} fusion(f32[4096,256]{1,0:T(8,128)} %convolution_multiply_fusion, s32[512]{0:T(512)S(1)} %bitcast.91, f32[512,256]{1,0:T(8,128)S(1)} %bitcast.84), kind=kCustom, calls=%fused_computation.8 | custom fusion | flops 131072 | bytes 1574912 | tf_op jit(solution)/shard_map/scatter-add | solution.py:99
  163.9 4.3 %convolution_multiply_fusion.1 = f32[512,256]{1,0:T(8,128)} fusion(bf16[4096,512]{1,0:T(8,128)(2,1)} %copy-done.1, bf16[4096,256]{1,0:T(8,128)(2,1)S(1)} %copy-done), kind=kOutput, calls=%fused_computation.27 | convolution fusion | flops 1073872896 | bytes 6815744 | tf_op jit(solution)/shard_map/dot_general | solution.py:109
  168.2 88.6 %all-reduce.6.cloned.1.call-done = (f32[4096,256]{1,0:T(8,128)}, f32[2048,256]{1,0:T(8,128)}, f32[64,256]{1,0:T(8,128)}) async-done(((f32[4096,256]{1,0:T(8,128)}, f32[2048,256]{1,0:T(8,128)}, f32[64,256]{1,0:T(8,128)}), (f32[4096,256]{1,0:T(8,128)}, f32[2048,256]{1,0:T(8,128)}, f32[64,256]{1,0:T(8,128)})) %all-reduce.6.cloned.1.call-update) | async-done | bytes 6357008 | tf_op jit(solution)/shard_map/psum | solution.py:113
  261.6 83.2 %all-reduce.4.cloned.1.call-done = f32[512,256]{1,0:T(8,128)} async-done(((f32[512,256]{1,0:T(8,128)}), f32[512,256]{1,0:T(8,128)}) %all-reduce.4.cloned.1.call-update) | async-done | bytes 524304 | tf_op jit(solution)/shard_map/psum | solution.py:112
  (89 shorter events, 40.5 us)
Async XLA Ops:
  7.2 42.2 %copy-start = (bf16[4096,256]{1,0:T(8,128)(2,1)S(1)}, bf16[4096,256]{1,0:T(8,128)(2,1)}, u32[]{:S(2)}) copy-start(bf16[4096,256]{1,0:T(8,128)(2,1)} %param.12) | copy-start | bytes 6291460
  7.2 52.2 %copy-start.2 = (bf16[2048,256]{1,0:T(8,128)(2,1)S(1)}, bf16[2048,256]{1,0:T(8,128)(2,1)}, u32[]{:S(2)}) copy-start(bf16[2048,256]{1,0:T(8,128)(2,1)} %param.13) | copy-start | bytes 3145732
  8.7 14.8 %all-to-all-start.2 = ((s32[16,1,4]{2,1,0:T(1,128)}), s32[16,1,4]{2,1,0:T(1,128)S(1)}, u32[]{:S(2)}, u32[]{:S(2)}) async-start(s32[16,1,4]{2,1,0:T(1,128)} %copy.36), calls=%async_computation.2 | async-start | bytes 16384 | tf_op jit(solution)/shard_map/all_to_all | solution.py:76
  23.5 12.6 %all-to-all-start = ((s32[16,1,32]{2,1,0:T(1,128)}), s32[16,1,32]{2,1,0:T(1,128)S(1)}, u32[]{:S(2)}, u32[]{:S(2)}) async-start(s32[16,1,32]{2,1,0:T(1,128)} %bitcast.92), calls=%async_computation | async-start | bytes 16384 | tf_op jit(solution)/shard_map/all_to_all | solution.py:74
  36.1 9.8 %all-to-all-start.4 = ((s32[16,1,32]{2,1,0:T(1,128)}), s32[16,1,32]{2,1,0:T(1,128)S(1)}, u32[]{:S(2)}, u32[]{:S(2)}) async-start(s32[16,1,32]{2,1,0:T(1,128)} %bitcast.93), calls=%async_computation.4 | async-start | bytes 16384 | tf_op jit(solution)/shard_map/all_to_all | solution.py:75
  45.8 9.9 %all-to-all-start.3 = ((bf16[16,4,256]{2,1,0:T(4,128)(2,1)}), bf16[16,4,256]{2,1,0:T(4,128)(2,1)S(1)}, u32[]{:S(2)}, u32[]{:S(2)}) async-start(bf16[16,4,256]{2,1,0:T(4,128)(2,1)} %reshape.426), calls=%async_computation.3 | async-start | bytes 65536 | tf_op jit(solution)/shard_map/all_to_all | solution.py:81
  55.8 10.8 %all-to-all-start.1 = ((bf16[16,32,256]{2,1,0:T(8,128)(2,1)}), bf16[16,32,256]{2,1,0:T(8,128)(2,1)S(1)}, u32[]{:S(2)}, u32[]{:S(2)}) async-start(bf16[16,32,256]{2,1,0:T(8,128)(2,1)} %bitcast.86), calls=%async_computation.1 | async-start | bytes 524288 | tf_op jit(solution)/shard_map/all_to_all | solution.py:79
  66.6 33.8 %all-to-all-start.5 = ((bf16[16,32,256]{2,1,0:T(8,128)(2,1)}), bf16[16,32,256]{2,1,0:T(8,128)(2,1)S(1)}, u32[]{:S(2)}, u32[]{:S(2)}) async-start(bf16[16,32,256]{2,1,0:T(8,128)(2,1)} %bitcast.85), calls=%async_computation.5 | async-start | bytes 524288 | tf_op jit(solution)/shard_map/all_to_all | solution.py:80
  106.0 1.8 copy-start.4
  109.2 13.2 %all-to-all-start.8 = ((f32[16,4,256]{2,1,0:T(4,128)}), f32[16,4,256]{2,1,0:T(4,128)S(1)}, u32[]{:S(2)}, u32[]{:S(2)}) async-start(f32[16,4,256]{2,1,0:T(4,128)} %reshape.407), calls=%async_computation.8 | async-start | bytes 131072 | tf_op jit(solution)/shard_map/all_to_all | solution.py:93
  115.8 13.2 %copy-start.3 = (bf16[512,256]{1,0:T(8,128)(2,1)S(1)}, bf16[512,256]{1,0:T(8,128)(2,1)}, u32[]{:S(2)}) copy-start(bf16[512,256]{1,0:T(8,128)(2,1)} %param.16) | copy-start | bytes 786436
  122.3 18.8 %all-to-all-start.7 = ((f32[16,32,256]{2,1,0:T(8,128)}), f32[16,32,256]{2,1,0:T(8,128)S(1)}, u32[]{:S(2)}, u32[]{:S(2)}) async-start(f32[16,32,256]{2,1,0:T(8,128)} %bitcast.33), calls=%async_computation.7 | async-start | bytes 1048576 | tf_op jit(solution)/shard_map/all_to_all | solution.py:92
  132.5 1.9 copy-start.1
  141.1 15.6 %all-to-all-start.6 = ((f32[16,32,256]{2,1,0:T(8,128)}), f32[16,32,256]{2,1,0:T(8,128)S(1)}, u32[]{:S(2)}, u32[]{:S(2)}) async-start(f32[16,32,256]{2,1,0:T(8,128)} %bitcast.29), calls=%async_computation.6 | async-start | bytes 1048576 | tf_op jit(solution)/shard_map/all_to_all | solution.py:91
  147.8 109.0 %all-reduce.6.cloned.1.call-start = ((), (), s32[]{:S(2)}) async-start(), calls=%async_computation.10 | async-start | bytes 12713984 | tf_op jit(solution)/shard_map/psum | solution.py:113
  163.9 181.0 %all-reduce.4.cloned.1.call-start = ((), (), s32[]{:S(2)}) async-start(), calls=%async_computation.9 | async-start | bytes 1048576 | tf_op jit(solution)/shard_map/psum | solution.py:112
Sparse Core Ops, SparseCore 0:
  164.0 92.7 all-reduce.5
  260.6 84.2 all-reduce.3
where the time goes:
time: 356 us; the launch traced here: 354 us
  waiting for transfers between devices  192 us (54%)
  local copies, waits for them, and re-layouts  58.7 us (16%)
  starting transfers between devices  48.7 us (14%)
  matrix products  20.7 us (6%)
  other arithmetic  19.2 us (5%)
  between operations  14.4 us (4%)
    psum x1, waiting for transfers between devices, local(): total_u, total_v, total_w = lax.psum((dense_u, dense_v, dense_w), 'narrow')  88.6 us
    psum x1, waiting for transfers between devices, local(): grad_features = lax.psum(feat_terms, 'wide')  83.2 us
    scatter x1, local copies, waits for them, and re-layouts, block_grads(): jnp.zeros((cells,), jnp.float32).at[pos].set(1.0)  18.9 us
    reshape x1, local copies, waits for them, and re-layouts, block_grads(): jnp.zeros((cells,), jnp.float32).at[pos].set(1.0)  9.43 us
    all_to_all x1, starting transfers between devices, local(): lax.all_to_all(week_need, 'wide', split_axis=0, concat_axis=0, tiled=True)  8.43 us
    scatter-add x1, other arithmetic, local(): jnp.zeros((own_users, RANK), jnp.float32).at[got_u.reshape(-1)]  7.15 us
  transfers between devices with their start and end apart: 11, of which 8 were waited for; matrix products, arithmetic and copies ran while one was open for 22% of the time, Pallas kernels for 0%

commit v1 on v0

v1 whole, which is shorter than its diff:
```python
import functools

import jax
import jax.numpy as jnp
from jax import lax
from jax.experimental import pallas as pl
from jax.experimental.pallas import tpu as pltpu
from jax.sharding import PartitionSpec as P

RANK = 256
BU = 256
BI = 256
BW = 28
CAPU = 32
CAPI = 32
CAPW = 4
CAPX = 16
MSG = CAPU + CAPI + CAPX
GROUP = 4
HALF = BW // 2
MESH = pl.DeviceIdType.MESH
F32, BF16, I32, I16 = jnp.float32, jnp.bfloat16, jnp.int32, jnp.int16


def dot(a, b):
    return jnp.dot(a, b, preferred_element_type=F32)


def dot_nt(a, b):
    return lax.dot_general(a, b, (((1,), (1,)), ((), ())), preferred_element_type=F32)


def dot_tn(a, b):
    return lax.dot_general(a, b, (((0,), (0,)), ((), ())), preferred_element_type=F32)


def iota(shape, axis):
    return lax.broadcasted_iota(I32, shape, axis)


def flat_index(counts, owners, place, cap):
    flat, end = place, 0
    for o in range(owners):
        c = counts[0, o]
        end = end + c
        flat = flat + jnp.where(place >= end, cap - c, 0)
    return flat


def halves(q):
    high = jnp.round(q * (1.0 / 256.0))
    return high, q - 256.0 * high


def kernel(
    W,
    NY,
    utab,
    itab,
    wtab,
    prof,
    ftab,
    reqs,
    ucnt,
    icnt,
    wcnt,
    pos,
    out_u,
    out_i,
    out_w,
    out_f,
    uv,
    iv,
    wv,
    xv,
    fv,
    x2,
    f2,
    rq,
    hot,
    rowsend,
    rowbuf,
    gp,
    pring,
    feat,
    fsend,
    frecv,
    fall,
    pos_s,
    near,
    keep,
    cacc,
    bits,
    uf,
    wf,
    vb,
    vt,
    gu,
    gv,
    gw,
    msg,
    mbuf,
    sbuf,
    accu,
    acci,
    accw,
    load_sem,
    req_ss,
    req_rs,
    x_ss,
    x_rs,
    row_ss,
    row_rs,
    fr_ss,
    fr_rs,
    fa_ss,
    fa_rs,
    pr_ss,
    pr_rs,
    ms_ss,
    ms_rs,
    ring_ss,
    ring_rs,
    sib_ss,
    sib_rs,
):
    me = lax.axis_index("wide")
    nar = lax.axis_index("narrow")
    y, c = nar // 2, nar % 2
    step = 1 - 2 * c
    nxt = lax.rem(y + step + NY, NY) * 2 + c
    prv = lax.rem(y - step + NY, NY) * 2 + c
    sib = y * 2 + 1 - c
    UR, IR, WR = uv.shape[0], iv.shape[0], wv.shape[0]
    FD = fv.shape[0]
    US, IS, WS = UR // (2 * NY), IR // (2 * NY), WR // (2 * NY)
    FC = FD // W

    def wrap(a):
        return lax.rem(a + W, W)

    def rcopy(src, dst, ss, rs, dev):
        return pltpu.make_async_remote_copy(
            src_ref=src,
            dst_ref=dst,
            send_sem=ss,
            recv_sem=rs,
            device_id=dev,
            device_id_type=MESH,
        )

    def peers(fn):
        lax.fori_loop(1, W, lambda s, z: (fn(s), z)[1], 0)

    loads = [
        pltpu.make_async_copy(utab, uv, load_sem.at[0]),
        pltpu.make_async_copy(itab, iv, load_sem.at[1]),
        pltpu.make_async_copy(wtab, wv, load_sem.at[2]),
        pltpu.make_async_copy(ftab, fv, load_sem.at[3]),
        pltpu.make_async_copy(prof, xv, load_sem.at[4]),
    ]
    for cp in loads:
        cp.start()
    barrier = pltpu.get_barrier_semaphore()
    peers(
        lambda s: pl.semaphore_signal(
            barrier, inc=1, device_id={"wide": wrap(me + s)}, device_id_type=MESH
        )
    )
    for n in (nxt, prv, sib):
        pl.semaphore_signal(barrier, inc=1, device_id={"narrow": n}, device_id_type=MESH)
    pl.semaphore_wait(barrier, W - 1 + 3)

    def req_copy(s):
        return rcopy(
            reqs.at[wrap(me + s)],
            rq.at[s],
            req_ss.at[s],
            req_rs.at[s],
            {"wide": wrap(me + s)},
        )

    peers(lambda s: req_copy(s).start())
    rq[0] = reqs[me]

    def x_copy(q):
        row = pl.multiple_of((2 * q + 1 - c) * US, US)
        return rcopy(
            prof.at[pl.ds(row, US), :], x2.at[q], x_ss.at[q], x_rs.at[q], {"narrow": sib}
        )

    f_copy = rcopy(ftab, f2, x_ss.at[NY], x_rs.at[NY], {"narrow": sib})
    f_copy.start()
    for q in range(NY):
        x_copy(q).start()

    for cp in loads[:3]:
        cp.wait()
    peers(lambda s: req_copy(s).wait_recv())
    RT = jnp.swapaxes(rq[...].reshape(W * 8, 128), 0, 1)

    def row_copy(s):
        return rcopy(
            rowsend.at[s],
            rowbuf.at[me],
            row_ss.at[s],
            row_rs.at[s],
            {"wide": wrap(me - s)},
        )

    part = W // 2
    for m in range(2):
        slots = range(m * part, (m + 1) * part)
        for table, kind, cap, first in ((uv, 0, CAPU, 0), (iv, 1, CAPI, CAPU), (wv, 2, CAPX, CAPU + CAPI)):
            rows = table.shape[0]
            for a, s in enumerate(slots):
                col = jnp.broadcast_to(RT[0:cap, 8 * s + kind : 8 * s + kind + 1], (cap, rows))
                hot[a * cap : (a + 1) * cap, 0:rows] = jnp.where(
                    col == iota((cap, rows), 1), 1.0, 0.0
                ).astype(BF16)
            got = dot(hot[0 : part * cap, 0:rows], table[...]).astype(BF16)
            rowsend[m * part : (m + 1) * part, first : first + cap, :] = got.reshape(part, cap, RANK)
        for s in slots:
            if s > 0:
                row_copy(s).start()
    rowbuf[me] = rowsend[0]

    for cp in loads[3:]:
        cp.wait()
    feat[...] = jnp.zeros_like(feat)

    def resid(row, x, f):
        return (dot_nt(uv[pl.ds(row, US), :], f) - x.astype(F32)).astype(BF16)

    def own_rows(q, z):
        row = pl.multiple_of((2 * q + c) * US, US)
        r = resid(row, xv[pl.ds(row, US), :], fv[...])
        feat[...] += dot_tn(uv[pl.ds(row, US), :], r)
        gp[q] = 0.0625 * dot(r, fv[...])
        row = pl.multiple_of((2 * q + 1 - c) * US, US)
        r = resid(row, xv[pl.ds(row, US), :], fv[...])
        feat[...] += dot_tn(uv[pl.ds(row, US), :], r)
        return z

    lax.fori_loop(0, NY, own_rows, 0)
    fsend[...] = (0.0625 * jnp.swapaxes(feat[...], 0, 1)).reshape(W, FC, RANK)

    def fr_copy(s):
        return rcopy(
            fsend.at[wrap(me + s)],
            frecv.at[s],
            fr_ss.at[s],
            fr_rs.at[s],
            {"wide": wrap(me + s)},
        )

    peers(lambda s: fr_copy(s).start())
    frecv[0] = fsend[me]
    f_copy.wait_recv()
    for q in range(NY):
        x_copy(q).wait_recv()

    def sib_rows(q, z):
        row = pl.multiple_of((2 * q + c) * US, US)
        gp[q] += 0.0625 * dot(resid(row, x2[q], f2[...]), f2[...])
        return z

    lax.fori_loop(0, NY, sib_rows, 0)

    def pr_copy(h):
        src = gp.at[lax.rem(y - step + NY, NY)] if h == 0 else pring.at[h - 1]
        return rcopy(src, pring.at[h], pr_ss.at[h], pr_rs.at[h], {"narrow": nxt})

    def pr_hop(h):
        pr_copy(h - 1).wait_recv()
        q = lax.rem(y - (h + 1) * step + 2 * NY, NY)
        pring[h - 1] += gp[q]
        if h < NY - 1:
            pr_copy(h).start()

    pr_copy(0).start()

    for k in range(32):
        pos_s[k : k + 1, :] = pos[:, 128 * k : 128 * (k + 1)]
    big = 1 << 30
    near[...] = jnp.full(near.shape, big, I32)
    pt = jnp.swapaxes(
        jnp.concatenate([pos_s[...], jnp.zeros((96, 128), I32)], axis=0), 0, 1
    )
    for k in range(32):
        mb = jnp.broadcast_to(pt[:, k : k + 1], (128, 128))
        x = jnp.where(iota((128, 128), 0) < iota((128, 128), 1), mb ^ pos_s[k : k + 1, :], big)
        best = near[k]
        for t in range(16):
            best = jnp.minimum(best, x[8 * t : 8 * t + 8, :])
        near[k] = best

        def later(n, z, mb=mb):
            row = jnp.broadcast_to(pos_s[pl.ds(n, 1), :], (8, 128))
            best = near[n]
            for t in range(16):
                best = jnp.minimum(best, mb[8 * t : 8 * t + 8, :] ^ row)
            near[n] = best
            return z

        lax.fori_loop(k + 1, 32, later, 0)
    for k in range(32):
        keep[:, 128 * k : 128 * (k + 1)] = jnp.min(near[k].astype(F32), axis=0, keepdims=True)
    cacc[...] = jnp.zeros_like(cacc)

    def mark(n, z):
        at = pl.ds(pl.multiple_of(n * 512, 512), 512)
        p = pos[:, at]
        week, user, item = p >> 16, (p >> 8) & 255, p & 255
        late = week >= HALF
        bit = jnp.left_shift(jnp.ones_like(week), jnp.where(late, week - HALF, week))
        w = jnp.where(keep[:, at] > 0.5, bit.astype(F32), 0.0)
        row = iota((256, 512), 0)
        mine = row == user
        a0 = jnp.where(mine, jnp.where(late, 0.0, w), 0.0).astype(BF16)
        a1 = jnp.where(mine, jnp.where(late, w, 0.0), 0.0).astype(BF16)
        b = jnp.where(row == item, 1.0, 0.0).astype(BF16)
        cacc[...] += dot_nt(jnp.concatenate([a0, a1], axis=0), b)
        return z

    lax.fori_loop(0, pos.shape[1] // 512, mark, 0)
    bits[...] = cacc[0:BU, :].astype(I32) | (cacc[BU : 2 * BU, :].astype(I32) << HALF)

    def pick(counts, n, cap):
        flat = flat_index(counts, W, iota((n, 1), 0), cap)
        return jnp.where(flat == iota((n, W * cap), 1), 1.0, 0.0).astype(BF16)

    pu, pv, pw = pick(ucnt, BU, CAPU), pick(icnt, BI, CAPI), pick(wcnt, 32, CAPX)

    def row_wait(s):
        rcopy(
            rowsend.at[s],
            rowbuf.at[wrap(me + s)],
            row_ss.at[s],
            row_rs.at[s],
            {"wide": wrap(me - s)},
        ).wait_recv()

    peers(row_wait)
    uf[...] = dot(pu, rowbuf[:, 0:CAPU, :].reshape(W * CAPU, RANK))
    vf = dot(pv, rowbuf[:, CAPU : CAPU + CAPI, :].reshape(W * CAPI, RANK))
    wf[...] = dot(pw, rowbuf[:, CAPU + CAPI : MSG, :].reshape(W * CAPX, RANK))
    vb[...] = vf.astype(BF16)
    vt[...] = jnp.swapaxes(vf, 0, 1).astype(BF16)
    gu[...] = jnp.zeros_like(gu)
    gv[...] = jnp.zeros_like(gv)
    gw[...] = jnp.zeros_like(gw)

    def week(k):
        w = wf[pl.ds(k, 1), :]
        uw = (uf[...] * w).astype(BF16)
        m = dot(uw, vt[...])
        hit = ((bits[...] >> k) & 1).astype(F32)
        g = (0.5 * jnp.tanh(0.5 * m) + (0.5 - hit)).astype(BF16)
        q = dot(g, vb[...])
        gu[...] += q * w
        gw[pl.ds(k, 1), :] = jnp.sum(q * uf[...], axis=0, keepdims=True)
        gv[...] += dot_tn(g, uw)

    def weeks(lo, hi):
        def two(k, z):
            week(2 * k)
            week(2 * k + 1)
            return z

        lax.fori_loop(lo // 2, hi // 2, two, 0)

    weeks(0, 10)
    pr_hop(1)

    peers(lambda s: fr_copy(s).wait_recv())
    total = frecv[0]
    for s in range(1, W):
        total = total + frecv[s]
    fall[me] = total

    def fa_copy(s):
        return rcopy(fall.at[me], fall.at[me], fa_ss.at[s], fa_rs.at[s], {"wide": wrap(me + s)})

    peers(lambda s: fa_copy(s).start())
    weeks(10, 20)
    pr_hop(2)
    weeks(20, BW)

    def encode(g, counts, cap):
        n = g.shape[0]
        top = jnp.maximum(jnp.max(jnp.abs(g), axis=1, keepdims=True), 2.0**-100)
        e = jnp.ceil(jnp.log2(top)) - 15.0
        q = jnp.clip(jnp.round(g * jnp.exp2(-e)), -32767.0, 32767.0)
        high, low = halves(q)
        rhs = jnp.concatenate([high, low, jnp.broadcast_to(e, (n, 128))], axis=1).astype(BF16)
        flat = flat_index(counts, W, iota((1, n), 1), cap)
        sel = jnp.where(flat == iota((W * cap, n), 0), 1.0, 0.0).astype(BF16)
        got = dot(sel, rhs)
        code = (256.0 * got[:, 0:RANK] + got[:, RANK : 2 * RANK]).astype(I32)
        es = got[:, 2 * RANK :].reshape(W, cap, 128)
        es = jnp.where(iota((W, cap, 128), 1) == iota((W, cap, 128), 2) % cap, es, 0.0)
        es = jnp.sum(es, axis=1, keepdims=True).astype(I32)
        return code.reshape(W, cap, RANK), es

    ucode, ue = encode(gu[...], ucnt, CAPU)
    msg[:, 0:CAPU, :] = ucode.astype(I16)
    vcode, ve = encode(gv[...], icnt, CAPI)
    msg[:, CAPU : CAPU + CAPI, :] = vcode.astype(I16)
    wcode, we = encode(gw[...], wcnt, CAPX)
    shape = (W, CAPX, RANK)
    none = jnp.zeros_like(we)
    tail = wcode
    for r, left, right in (
        (8, reqs[:, 0:1, :], reqs[:, 1:2, :]),
        (9, reqs[:, 2:3, :], none),
        (10, ue, ve),
        (11, we, none),
    ):
        line = jnp.broadcast_to(jnp.concatenate([left, right], axis=2), shape)
        tail = jnp.where(iota(shape, 1) == r, line, tail)
    msg[:, CAPU + CAPI : MSG, :] = tail.astype(I16)

    def ms_copy(s):
        return rcopy(
            msg.at[wrap(me + s)],
            mbuf.at[0, s],
            ms_ss.at[s],
            ms_rs.at[s],
            {"wide": wrap(me + s)},
        )

    peers(lambda s: ms_copy(s).start())
    mbuf[0, 0] = msg[me]

    groups = W // GROUP

    def span(g):
        return pl.ds(g * GROUP, GROUP)

    def ring_copy(h, g):
        return rcopy(
            mbuf.at[h, span(g)],
            mbuf.at[h + 1, span(g)],
            ring_ss.at[h, g],
            ring_rs.at[h, g],
            {"narrow": nxt},
        )

    def sib_copy(h, g):
        return rcopy(
            mbuf.at[h, span(g)],
            sbuf.at[h, span(g)],
            sib_ss.at[h, g],
            sib_rs.at[h, g],
            {"narrow": sib},
        )

    share = nar
    accu[...] = jnp.zeros_like(accu)
    acci[...] = jnp.zeros_like(acci)
    accw[...] = jnp.zeros_like(accw)

    def lanes(tail_rows, r, first, cap):
        each = 128 // cap
        pieces = []
        for p in range(W // each):
            piece = jnp.zeros((1, 128), F32)
            for a in range(each):
                line = tail_rows[p * each + a, r : r + 1, first : first + 128]
                piece = jnp.where(iota((1, 128), 1) // cap == a, line, piece)
            pieces.append(piece)
        return jnp.concatenate(pieces, axis=1)

    def add_rows(buf, h):
        tail_rows = buf[h, :, CAPU + CAPI : MSG, :].astype(I32).astype(F32)
        for acc, kind, lo, cap, size in (
            (accu, 0, 0, CAPU, US),
            (acci, 1, CAPU, CAPI, IS),
            (accw, 2, CAPU + CAPI, CAPX, WS),
        ):
            r, first = (8, 128 * kind) if kind < 2 else (9, 0)
            ids = lanes(tail_rows, r, first, cap)
            scale = jnp.exp2(lanes(tail_rows, r + 2, first, cap))
            rows = acc.shape[0]
            place = (iota((rows, W * cap), 0) + share * size).astype(F32)
            sel = jnp.where(ids == place, jnp.broadcast_to(scale, place.shape), 0.0).astype(BF16)
            q = buf[h, :, lo : lo + cap, :].astype(I32).astype(F32)
            if kind == 2:
                q = jnp.where(iota(q.shape, 1) < CAPW, q, 0.0)
            high, low = halves(q.reshape(W * cap, RANK))
            acc[...] += dot(sel, jnp.concatenate([high, low], axis=1).astype(BF16))

    for g in range(groups):
        for s in range(g * GROUP, (g + 1) * GROUP):
            if s > 0:
                ms_copy(s).wait_recv()
        ring_copy(0, g).start()
        sib_copy(0, g).start()
    pr_hop(3)

    def fa_wait(s):
        rcopy(
            fall.at[me],
            fall.at[wrap(me - s)],
            fa_ss.at[s],
            fa_rs.at[s],
            {"wide": wrap(me + s)},
        ).wait_recv()

    peers(fa_wait)
    out_f[...] = fall[...].reshape(FD, RANK)
    add_rows(mbuf, 0)
    for h in range(1, NY):
        for g in range(groups):
            ring_copy(h - 1, g).wait_recv()
            if h < NY - 1:
                ring_copy(h, g).start()
            sib_copy(h, g).start()
        for g in range(groups):
            sib_copy(h - 1, g).wait_recv()
        add_rows(sbuf, h - 1)
        add_rows(mbuf, h)
    for g in range(groups):
        sib_copy(NY - 1, g).wait_recv()
    add_rows(sbuf, NY - 1)

    out_u[...] = 256.0 * accu[:, 0:RANK] + accu[:, RANK:] + pring[NY - 2]
    out_i[...] = 256.0 * acci[:, 0:RANK] + acci[:, RANK:]
    out_w[...] = 256.0 * accw[0:WS, 0:RANK] + accw[0:WS, RANK:]

    def sent(s):
        req_copy(s).wait_send()
        row_copy(s).wait_send()
        fr_copy(s).wait_send()
        fa_copy(s).wait_send()
        ms_copy(s).wait_send()

    peers(sent)
    f_copy.wait_send()
    for q in range(NY):
        x_copy(q).wait_send()
    for h in range(NY - 1):
        pr_copy(h).wait_send()
        for g in range(groups):
            ring_copy(h, g).wait_send()
    for h in range(NY):
        for g in range(groups):
            sib_copy(h, g).wait_send()


def local(
    W,
    NY,
    user_table,
    item_table,
    week_table,
    profile,
    feature_table,
    user_req,
    item_req,
    week_req,
    user_counts,
    item_counts,
    week_counts,
    pos_cells,
):
    lines = jnp.stack(
        [
            jnp.tile(user_req[0], (1, 128 // CAPU)),
            jnp.tile(item_req[0], (1, 128 // CAPI)),
            jnp.tile(jnp.pad(week_req[0], ((0, 0), (0, CAPX - CAPW))), (1, 128 // CAPX)),
        ],
        axis=1,
    )
    reqs = jnp.pad(lines, ((0, 0), (0, 5), (0, 0)))
    UR, IR, WR = user_table.shape[0], item_table.shape[0], week_table.shape[0]
    FD = feature_table.shape[0]
    US, IS, WS = UR // (2 * NY), IR // (2 * NY), WR // (2 * NY)
    FC = FD // W
    groups = W // GROUP
    V, D = pltpu.VMEM, pltpu.SemaphoreType.DMA
    anywhere = pl.BlockSpec(memory_space=pl.ANY)
    vmem = pl.BlockSpec(memory_space=pltpu.VMEM)
    smem = pl.BlockSpec(memory_space=pltpu.SMEM)
    return pl.pallas_call(
        functools.partial(kernel, W, NY),
        out_shape=(
            jax.ShapeDtypeStruct((US, RANK), F32),
            jax.ShapeDtypeStruct((IS, RANK), F32),
            jax.ShapeDtypeStruct((WS, RANK), F32),
            jax.ShapeDtypeStruct((FD, RANK), F32),
        ),
        in_specs=[anywhere] * 5 + [vmem] + [smem] * 3 + [vmem],
        out_specs=(vmem, vmem, vmem, vmem),
        scratch_shapes=[
            V((UR, RANK), BF16),
            V((IR, RANK), BF16),
            V((WR, RANK), BF16),
            V((UR, FD), BF16),
            V((FD, RANK), BF16),
            V((NY, US, FD), BF16),
            V((FD, RANK), BF16),
            V((W, 8, 128), I32),
            V((W // 2 * CAPU, UR), BF16),
            V((W, MSG, RANK), BF16),
            V((W, MSG, RANK), BF16),
            V((NY, US, RANK), F32),
            V((NY - 1, US, RANK), F32),
            V((RANK, FD), F32),
            V((W, FC, RANK), F32),
            V((W, FC, RANK), F32),
            V((W, FC, RANK), F32),
            V((32, 128), I32),
            V((32, 8, 128), I32),
            V((1, pos_cells.shape[1]), F32),
            V((2 * BU, BI), F32),
            V((BU, BI), I32),
            V((BU, RANK), F32),
            V((32, RANK), F32),
            V((BI, RANK), BF16),
            V((RANK, BI), BF16),
            V((BU, RANK), F32),
            V((BI, RANK), F32),
            V((32, RANK), F32),
            V((W, MSG, RANK), I16),
            V((NY, W, MSG, RANK), I16),
            V((NY, W, MSG, RANK), I16),
            V((US, 2 * RANK), F32),
            V((IS, 2 * RANK), F32),
            V((16, 2 * RANK), F32),
            D((5,)),
            D((W,)),
            D((W,)),
            D((NY + 1,)),
            D((NY + 1,)),
            D((W,)),
            D((W,)),
            D((W,)),
            D((W,)),
            D((W,)),
            D((W,)),
            D((NY - 1,)),
            D((NY - 1,)),
            D((W,)),
            D((W,)),
            D((NY - 1, groups)),
            D((NY - 1, groups)),
            D((NY, groups)),
            D((NY, groups)),
        ],
        compiler_params=pltpu.CompilerParams(
            collective_id=0, has_side_effects=True, vmem_limit_bytes=56 << 20
        ),
    )(
        user_table,
        item_table,
        week_table,
        profile,
        feature_table,
        reqs,
        user_counts,
        item_counts,
        week_counts,
        pos_cells,
    )


def solution(mesh):
    W, NY = mesh.shape["wide"], mesh.shape["narrow"] // 2
    both = ("wide", "narrow")
    return jax.shard_map(
        functools.partial(local, W, NY),
        mesh=mesh,
        in_specs=(
            P("wide", None),
            P("wide", None),
            P("wide", None),
            P("wide", "narrow"),
            P("narrow", None),
            P(both, None, None),
            P(both, None, None),
            P(both, None, None),
            P(both, None),
            P(both, None),
            P(both, None),
            P(both, None),
        ),
        out_specs=(P(both, None), P(both, None), P(both, None), P("narrow", None)),
        check_vma=False,
    )
```

time: 356 us -> 103 us (0.29)
  waiting for transfers between devices: 192 us -> 0 us
  Pallas kernels: 0 us -> 91.8 us
  local copies, waits for them, and re-layouts: 58.7 us -> 9.79 us
  starting transfers between devices: 48.7 us -> 0 us
  matrix products: 20.7 us -> 0 us
  other arithmetic: 19.2 us -> 0.03 us
  between operations: 14.4 us -> 0.66 us
    psum x2 -> x0, waiting for transfers between devices: 172 us -> none  [the longest x1 88.6 us: local(): total_u, total_v, total_w = lax.psum((dense_u, dense_v, dense_w), 'narrow')]
    pallas_call x0 -> x1, Pallas kernels: none -> 91.8 us  [local(): pl.pallas_call(functools.partial(kernel, W, NY), out_shape=(jax.ShapeDtyp...]
    all_to_all x9 -> x0, starting transfers between devices: 48.6 us -> none  [the longest x1 8.43 us: local(): lax.all_to_all(week_need, 'wide', split_axis=0, concat_axis=0, tiled=True)]
    scatter x4 -> x0, local copies, waits for them, and re-layouts: 24.4 us -> none  [the longest x1 18.9 us: block_grads(): jnp.zeros((cells,), jnp.float32).at[pos].set(1.0)]
    dot_general x6 -> x0, matrix products: 20.7 us -> none  [the longest x1 4.45 us: block_grads(): jnp.einsum('kir,jr->kij', mixed, item_rows, preferred_element_type=jnp.fl...]
    all_to_all x9 -> x0, waiting for transfers between devices: 20.1 us -> none  [the longest x1 6.18 us: local(): lax.all_to_all(item_need, 'wide', split_axis=0, concat_axis=0, tiled=True)]
    scatter-add x3 -> x0, other arithmetic: 13.4 us -> none  [the longest x1 7.15 us: local(): jnp.zeros((own_users, RANK), jnp.float32).at[got_u.reshape(-1)]]
    reshape x8 -> x0, local copies, waits for them, and re-layouts: 11.1 us -> none  [the longest x1 9.43 us: block_grads(): jnp.zeros((cells,), jnp.float32).at[pos].set(1.0)]
  transfers between devices with their start and end apart: 11 -> 0, of which waited for: 8 -> 0; matrix products, arithmetic and copies ran while one was open for 22% -> 0% of each run, Pallas kernels for 0% -> 0%
where the time goes in v1:
time: 103 us; the launch traced here: 102 us
  Pallas kernels  91.8 us (89%)
  local copies, waits for them, and re-layouts  9.79 us (10%)
    pallas_call x1, Pallas kernels, local(): pl.pallas_call(functools.partial(kernel, W, NY), out_shape=(jax.ShapeDtyp...  91.8 us
    unnamed x5, local copies, waits for them, and re-layouts  7.46 us

profile of v1, /device:TPU:1, one launch (start us, length us, event | category | flops | bytes accessed | tf_op | source)
XLA Modules:
  0.0 102.3 jit_solution(9395469419106027442)
XLA Ops:
  0.6 0.8 copy.17
  1.4 0.7 tile.27
  2.1 0.1 tile.28
  2.2 0.7 tile.30
  2.9 0.1 tile.31
  3.0 0.1 tile.33
  3.1 0.6 pad.9.reqs
  3.8 91.8 %shard_map.147 = (f32[512,256]{1,0:T(8,128)}, f32[256,256]{1,0:T(8,128)}, f32[8,256]{1,0:T(8,128)}, f32[512,256]{1,0:T(8,128)}) custom-call(bf16[4096,256]{1,0:T(8,128)(2,1)} %utab.1, bf16[2048,256]{1,0:T(8,128)(2,1)} %itab.1, bf16[64,256]{1,0:T(8,128)(2,1)} %wtab.1, bf16[4096,512]{1,0:T(8,128)(2,1)} %prof.1, bf16[512,256]{1,0:T(8,128)(2,1)} %ftab.1, ...), custom_call_target="tpu_custom_call" | custom-call | tf_op jit(solution)/shard_map/pallas_call | solution.py:586
  95.6 1.9 %copy.22 = f32[512,256]{1,0:T(8,128)} copy(f32[512,256]{1,0:T(8,128)} %get-tuple-element.8) | data formatting | bytes 1048576
  97.5 1.7 %copy.23 = f32[256,256]{1,0:T(8,128)} copy(f32[256,256]{1,0:T(8,128)} %get-tuple-element.9) | data formatting | bytes 524288
  99.1 1.3 %copy.24 = f32[8,256]{1,0:T(8,128)} copy(f32[8,256]{1,0:T(8,128)} %get-tuple-element.10) | data formatting | bytes 16384
  100.4 1.9 %copy.25 = f32[512,256]{1,0:T(8,128)} copy(f32[512,256]{1,0:T(8,128)} %get-tuple-element.11) | data formatting | bytes 1048576
  (3 shorter events, 0.0 us)

commit v2 on v1

--- a/solution.py
+++ b/solution.py
@@ -17,7 +17,13 @@
 CAPX = 16
 MSG = CAPU + CAPI + CAPX
 GROUP = 4
-HALF = BW // 2
+GROUPS = (0, 1, 3, 2)
+FIELDS = 12
+BLOCK = 4
+THIRD = 3
+PAIR = 2
+SIDE = 4
+ORDER = (1, 4, 3, 12, 5, 15, 7, 13, 2, 8, 9, 14, 11, 6, 10)
 MESH = pl.DeviceIdType.MESH
 F32, BF16, I32, I16 = jnp.float32, jnp.bfloat16, jnp.int32, jnp.int16
 
@@ -50,6 +56,14 @@
 def halves(q):
     high = jnp.round(q * (1.0 / 256.0))
     return high, q - 256.0 * high
+
+
+def exponent(top):
+    return jnp.ceil(jnp.log2(jnp.maximum(top, 2.0**-100))) - 15.0
+
+
+def quantize(x, e):
+    return jnp.clip(jnp.round(x * jnp.exp2(-e)), -32767.0, 32767.0)
 
 
 def kernel(
@@ -60,7 +74,9 @@
     wtab,
     prof,
     ftab,
-    reqs,
+    ureq,
+    ireq,
+    wreq,
     ucnt,
     icnt,
     wcnt,
@@ -76,11 +92,13 @@
     fv,
     x2,
     f2,
+    reqs,
     rq,
     hot,
     rowsend,
     rowbuf,
     gp,
+    prsend,
     pring,
     feat,
     fsend,
@@ -89,6 +107,7 @@
     pos_s,
     near,
     keep,
+    spread,
     cacc,
     bits,
     uf,
@@ -98,6 +117,12 @@
     gu,
     gv,
     gw,
+    uw0,
+    uw1,
+    mm0,
+    mm1,
+    gg0,
+    gg1,
     msg,
     mbuf,
     sbuf,
@@ -136,8 +161,13 @@
     US, IS, WS = UR // (2 * NY), IR // (2 * NY), WR // (2 * NY)
     FC = FD // W
 
-    def wrap(a):
-        return lax.rem(a + W, W)
+    X, Z = me // SIDE, lax.rem(me, SIDE)
+
+    def to(s):
+        return lax.rem(X + s // SIDE, SIDE) * SIDE + lax.rem(Z + s % SIDE, SIDE)
+
+    def frm(s):
+        return lax.rem(X + SIDE - s // SIDE, SIDE) * SIDE + lax.rem(Z + SIDE - s % SIDE, SIDE)
 
     def rcopy(src, dst, ss, rs, dev):
         return pltpu.make_async_remote_copy(
@@ -150,7 +180,10 @@
         )
 
     def peers(fn):
-        lax.fori_loop(1, W, lambda s, z: (fn(s), z)[1], 0)
+        for s in ORDER:
+            fn(s)
+
+    leave, pend = [], {}
 
     loads = [
         pltpu.make_async_copy(utab, uv, load_sem.at[0]),
@@ -161,27 +194,41 @@
     ]
     for cp in loads:
         cp.start()
+    pend["tables"] = lambda: [cp.wait() for cp in loads[:3]]
+    pend["profile"] = lambda: [cp.wait() for cp in loads[3:]]
     barrier = pltpu.get_barrier_semaphore()
     peers(
         lambda s: pl.semaphore_signal(
-            barrier, inc=1, device_id={"wide": wrap(me + s)}, device_id_type=MESH
+            barrier, inc=1, device_id={"wide": to(s)}, device_id_type=MESH
         )
     )
     for n in (nxt, prv, sib):
         pl.semaphore_signal(barrier, inc=1, device_id={"narrow": n}, device_id_type=MESH)
+    for kind, ids in ((0, ureq[...]), (1, ireq[...])):
+        line = jnp.concatenate([ids] * (128 // ids.shape[1]), axis=1)
+        for o in range(W):
+            reqs[o, kind : kind + 1, :] = line[o : o + 1, :]
+    used = jnp.concatenate([wreq[...], jnp.zeros((CAPX - CAPW, W), I32)], axis=0)
+    used = jnp.concatenate([used] * (128 // CAPX), axis=0)
+    used = jnp.swapaxes(jnp.concatenate([used] * (128 // W), axis=1), 0, 1)
+    for o in range(W):
+        reqs[o, 2:3, :] = used[o : o + 1, :]
+        reqs[o, 3:8, :] = jnp.zeros((5, 128), I32)
     pl.semaphore_wait(barrier, W - 1 + 3)
 
     def req_copy(s):
         return rcopy(
-            reqs.at[wrap(me + s)],
+            reqs.at[to(s)],
             rq.at[s],
             req_ss.at[s],
             req_rs.at[s],
-            {"wide": wrap(me + s)},
+            {"wide": to(s)},
         )
 
     peers(lambda s: req_copy(s).start())
     rq[0] = reqs[me]
+    leave.append(lambda: peers(lambda s: req_copy(s).wait_send()))
+    pend["rq"] = lambda: peers(lambda s: req_copy(s).wait_recv())
 
     def x_copy(q):
         row = pl.multiple_of((2 * q + 1 - c) * US, US)
@@ -194,9 +241,61 @@
     for q in range(NY):
         x_copy(q).start()
 
-    for cp in loads[:3]:
-        cp.wait()
-    peers(lambda s: req_copy(s).wait_recv())
+    def x_wait():
+        f_copy.wait_recv()
+        for q in range(NY):
+            x_copy(q).wait_recv()
+
+    def x_sent():
+        f_copy.wait_send()
+        for q in range(NY):
+            x_copy(q).wait_send()
+
+    pend["x"] = x_wait
+    leave.append(x_sent)
+
+    big = 1 << 30
+
+    def least(xs):
+        while len(xs) > 1:
+            xs = [jnp.minimum(a, b) for a, b in zip(xs[::2], xs[1::2])]
+        return xs[0]
+
+    lines = pos.shape[1] // 128
+    for k in range(lines):
+        pos_s[k : k + 1, :] = pos[:, 128 * k : 128 * (k + 1)]
+    near[...] = jnp.full(near.shape, big, I32)
+    pt = jnp.swapaxes(
+        jnp.concatenate([pos_s[...], jnp.zeros((128 - lines, 128), I32)], axis=0), 0, 1
+    )
+    for k in range(lines):
+        spread[k] = jnp.broadcast_to(pt[:, k : k + 1], (128, 128))
+
+    def compare(k, block, masked):
+        for a in range(BLOCK):
+            n = block * BLOCK + a
+            row = jnp.broadcast_to(pos_s[pl.ds(n, 1), :], (8, 128))
+            xs = []
+            for t in range(16):
+                x = spread[k, 8 * t : 8 * t + 8, :] ^ row
+                if masked:
+                    first = k * 128 + 8 * t + iota((8, 128), 0)
+                    x = jnp.where(first < n * 128 + iota((8, 128), 1), x, big)
+                xs.append(x)
+            near[n] = jnp.minimum(near[n], least(xs))
+
+    def column(k, z):
+        own = k // BLOCK
+        stop = jnp.minimum((own // THIRD + 1) * THIRD, lines // BLOCK)
+        compare(k, own, True)
+        lax.fori_loop(own + 1, stop, lambda b, y: (compare(k, b, False), y)[1], 0)
+        return z
+
+    lax.fori_loop(0, lines, column, 0)
+    for k in range(lines):
+        keep[:, 128 * k : 128 * (k + 1)] = jnp.min(near[k].astype(F32), axis=0, keepdims=True)
+    pend.pop("tables")()
+    pend.pop("rq")()
     RT = jnp.swapaxes(rq[...].reshape(W * 8, 128), 0, 1)
 
     def row_copy(s):
@@ -205,7 +304,7 @@
             rowbuf.at[me],
             row_ss.at[s],
             row_rs.at[s],
-            {"wide": wrap(me - s)},
+            {"wide": frm(s)},
         )
 
     part = W // 2
@@ -220,13 +319,24 @@
                 ).astype(BF16)
             got = dot(hot[0 : part * cap, 0:rows], table[...]).astype(BF16)
             rowsend[m * part : (m + 1) * part, first : first + cap, :] = got.reshape(part, cap, RANK)
-        for s in slots:
-            if s > 0:
+        for s in ORDER:
+            if s in slots:
                 row_copy(s).start()
     rowbuf[me] = rowsend[0]
 
-    for cp in loads[3:]:
-        cp.wait()
+    def row_wait(s):
+        rcopy(
+            rowsend.at[s],
+            rowbuf.at[to(s)],
+            row_ss.at[s],
+            row_rs.at[s],
+            {"wide": frm(s)},
+        ).wait_recv()
+
+    leave.append(lambda: peers(lambda s: row_copy(s).wait_send()))
+    pend["row"] = lambda: peers(row_wait)
+
+    pend.pop("profile")()
     feat[...] = jnp.zeros_like(feat)
 
     def resid(row, x, f):
@@ -247,18 +357,18 @@
 
     def fr_copy(s):
         return rcopy(
-            fsend.at[wrap(me + s)],
+            fsend.at[to(s)],
             frecv.at[s],
             fr_ss.at[s],
             fr_rs.at[s],
-            {"wide": wrap(me + s)},
+            {"wide": to(s)},
         )
 
     peers(lambda s: fr_copy(s).start())
     frecv[0] = fsend[me]
-    f_copy.wait_recv()
-    for q in range(NY):
-        x_copy(q).wait_recv()
+    leave.append(lambda: peers(lambda s: fr_copy(s).wait_send()))
+    pend["fr"] = lambda: peers(lambda s: fr_copy(s).wait_recv())
+    pend.pop("x")()
 
     def sib_rows(q, z):
         row = pl.multiple_of((2 * q + c) * US, US)
@@ -268,63 +378,51 @@
     lax.fori_loop(0, NY, sib_rows, 0)
 
     def pr_copy(h):
-        src = gp.at[lax.rem(y - step + NY, NY)] if h == 0 else pring.at[h - 1]
-        return rcopy(src, pring.at[h], pr_ss.at[h], pr_rs.at[h], {"narrow": nxt})
+        return rcopy(prsend.at[h], pring.at[h], pr_ss.at[h], pr_rs.at[h], {"narrow": nxt})
+
+    def pr_start(h, x):
+        e = exponent(jnp.max(jnp.abs(x), axis=0, keepdims=True))
+        prsend[h, 0:US, :] = quantize(x, e).astype(I32).astype(I16)
+        prsend[h, US:, :] = jnp.broadcast_to(e, (16, RANK)).astype(I32).astype(I16)
+        pr_copy(h).start()
+        leave.append(lambda: pr_copy(h).wait_send())
+        pend["pr"] = lambda: pr_copy(h).wait_recv()
 
     def pr_hop(h):
-        pr_copy(h - 1).wait_recv()
+        pend.pop("pr")()
         q = lax.rem(y - (h + 1) * step + 2 * NY, NY)
-        pring[h - 1] += gp[q]
+        e = pring[h - 1, US:, :].astype(I32).astype(F32)[0:1, :]
+        x = pring[h - 1, 0:US, :].astype(I32).astype(F32) * jnp.exp2(e) + gp[q]
         if h < NY - 1:
-            pr_copy(h).start()
-
-    pr_copy(0).start()
-
-    for k in range(32):
-        pos_s[k : k + 1, :] = pos[:, 128 * k : 128 * (k + 1)]
-    big = 1 << 30
-    near[...] = jnp.full(near.shape, big, I32)
-    pt = jnp.swapaxes(
-        jnp.concatenate([pos_s[...], jnp.zeros((96, 128), I32)], axis=0), 0, 1
-    )
-    for k in range(32):
-        mb = jnp.broadcast_to(pt[:, k : k + 1], (128, 128))
-        x = jnp.where(iota((128, 128), 0) < iota((128, 128), 1), mb ^ pos_s[k : k + 1, :], big)
-        best = near[k]
-        for t in range(16):
-            best = jnp.minimum(best, x[8 * t : 8 * t + 8, :])
-        near[k] = best
-
-        def later(n, z, mb=mb):
-            row = jnp.broadcast_to(pos_s[pl.ds(n, 1), :], (8, 128))
-            best = near[n]
-            for t in range(16):
-                best = jnp.minimum(best, mb[8 * t : 8 * t + 8, :] ^ row)
-            near[n] = best
-            return z
-
-        lax.fori_loop(k + 1, 32, later, 0)
-    for k in range(32):
-        keep[:, 128 * k : 128 * (k + 1)] = jnp.min(near[k].astype(F32), axis=0, keepdims=True)
+            pr_start(h, x)
+        else:
+            gp[y] = x
+
+    pr_start(0, gp[lax.rem(y - step + NY, NY)])
+
     cacc[...] = jnp.zeros_like(cacc)
 
     def mark(n, z):
         at = pl.ds(pl.multiple_of(n * 512, 512), 512)
         p = pos[:, at]
         week, user, item = p >> 16, (p >> 8) & 255, p & 255
-        late = week >= HALF
-        bit = jnp.left_shift(jnp.ones_like(week), jnp.where(late, week - HALF, week))
+        part = week // FIELDS
+        bit = jnp.left_shift(jnp.ones_like(week), 2 * (week - FIELDS * part))
         w = jnp.where(keep[:, at] > 0.5, bit.astype(F32), 0.0)
         row = iota((256, 512), 0)
-        mine = row == user
-        a0 = jnp.where(mine, jnp.where(late, 0.0, w), 0.0).astype(BF16)
-        a1 = jnp.where(mine, jnp.where(late, w, 0.0), 0.0).astype(BF16)
+        mine = jnp.where(row == user, 1.0, 0.0).astype(BF16)
+        a = [mine * jnp.where(part == f, w, 0.0).astype(BF16) for f in range(3)]
         b = jnp.where(row == item, 1.0, 0.0).astype(BF16)
-        cacc[...] += dot_nt(jnp.concatenate([a0, a1], axis=0), b)
+        cacc[...] += dot_nt(jnp.concatenate(a, axis=0), b)
         return z
 
     lax.fori_loop(0, pos.shape[1] // 512, mark, 0)
-    bits[...] = cacc[0:BU, :].astype(I32) | (cacc[BU : 2 * BU, :].astype(I32) << HALF)
+
+    def present(f):
+        n = cacc[f * BU : (f + 1) * BU, :].astype(I32)
+        return (n | (n >> 1)) & 0x555555
+
+    bits[...] = present(0) | (present(1) << 1) | (present(2) << (2 * FIELDS))
 
     def pick(counts, n, cap):
         flat = flat_index(counts, W, iota((n, 1), 0), cap)
@@ -332,67 +430,81 @@
 
     pu, pv, pw = pick(ucnt, BU, CAPU), pick(icnt, BI, CAPI), pick(wcnt, 32, CAPX)
 
-    def row_wait(s):
-        rcopy(
-            rowsend.at[s],
-            rowbuf.at[wrap(me + s)],
-            row_ss.at[s],
-            row_rs.at[s],
-            {"wide": wrap(me - s)},
-        ).wait_recv()
-
-    peers(row_wait)
+    pend.pop("row")()
     uf[...] = dot(pu, rowbuf[:, 0:CAPU, :].reshape(W * CAPU, RANK))
     vf = dot(pv, rowbuf[:, CAPU : CAPU + CAPI, :].reshape(W * CAPI, RANK))
     wf[...] = dot(pw, rowbuf[:, CAPU + CAPI : MSG, :].reshape(W * CAPX, RANK))
-    vb[...] = vf.astype(BF16)
-    vt[...] = jnp.swapaxes(vf, 0, 1).astype(BF16)
+    vb[...] = (0.5 * vf).astype(BF16)
+    vt[...] = (0.5 * jnp.swapaxes(vf, 0, 1)).astype(BF16)
     gu[...] = jnp.zeros_like(gu)
     gv[...] = jnp.zeros_like(gv)
     gw[...] = jnp.zeros_like(gw)
 
-    def week(k):
-        w = wf[pl.ds(k, 1), :]
-        uw = (uf[...] * w).astype(BF16)
-        m = dot(uw, vt[...])
-        hit = ((bits[...] >> k) & 1).astype(F32)
-        g = (0.5 * jnp.tanh(0.5 * m) + (0.5 - hit)).astype(BF16)
-        q = dot(g, vb[...])
-        gu[...] += q * w
-        gw[pl.ds(k, 1), :] = jnp.sum(q * uf[...], axis=0, keepdims=True)
-        gv[...] += dot_tn(g, uw)
+    def lead(k, uw, mm):
+        for a in range(PAIR):
+            uw[BU * a : BU * (a + 1), :] = (uf[...] * wf[pl.ds(k + a, 1), :]).astype(BF16)
+        mm[...] = dot(uw[...], vt[...])
+
+    def work(k, uw, mm, gg):
+        place = jnp.where(k < FIELDS, 2 * k, jnp.where(k < 2 * FIELDS, 2 * (k - FIELDS) + 1, 2 * (k - FIELDS)))
+        hits = bits[...] >> place
+        for a in range(PAIR):
+            sign = jnp.where((hits & (1 << (2 * a))) != 0, -1.0, 1.0)
+            at = slice(BU * a, BU * (a + 1))
+            gg[at, :] = (jnp.tanh(mm[at, :]) + sign).astype(BF16)
+        q = dot(gg[...], vb[...])
+        total = gu[...]
+        for a in range(PAIR):
+            w, qa = wf[pl.ds(k + a, 1), :], q[BU * a : BU * (a + 1), :]
+            total = total + qa * w
+            gw[pl.ds(k + a, 1), :] = jnp.sum(qa * uf[...], axis=0, keepdims=True)
+        gu[...] = total
+        gv[...] += dot_tn(gg[...], uw[...])
 
     def weeks(lo, hi):
-        def two(k, z):
-            week(2 * k)
-            week(2 * k + 1)
+        def both(n, z):
+            k = 2 * PAIR * n
+            lead(k + PAIR, uw1, mm1)
+            work(k, uw0, mm0, gg0)
+            lead(k + 2 * PAIR, uw0, mm0)
+            work(k + PAIR, uw1, mm1, gg1)
             return z
 
-        lax.fori_loop(lo // 2, hi // 2, two, 0)
-
-    weeks(0, 10)
+        lax.fori_loop(lo // (2 * PAIR), hi // (2 * PAIR), both, 0)
+
+    lead(0, uw0, mm0)
+    weeks(0, 12)
     pr_hop(1)
 
-    peers(lambda s: fr_copy(s).wait_recv())
+    pend.pop("fr")()
     total = frecv[0]
     for s in range(1, W):
         total = total + frecv[s]
     fall[me] = total
 
     def fa_copy(s):
-        return rcopy(fall.at[me], fall.at[me], fa_ss.at[s], fa_rs.at[s], {"wide": wrap(me + s)})
+        return rcopy(fall.at[me], fall.at[me], fa_ss.at[s], fa_rs.at[s], {"wide": to(s)})
 
     peers(lambda s: fa_copy(s).start())
-    weeks(10, 20)
+
+    def fa_wait(s):
+        rcopy(
+            fall.at[me],
+            fall.at[frm(s)],
+            fa_ss.at[s],
+            fa_rs.at[s],
+            {"wide": to(s)},
+        ).wait_recv()
+
+    leave.append(lambda: peers(lambda s: fa_copy(s).wait_send()))
+    pend["fa"] = lambda: peers(fa_wait)
+    weeks(12, BW)
     pr_hop(2)
-    weeks(20, BW)
 
     def encode(g, counts, cap):
         n = g.shape[0]
-        top = jnp.maximum(jnp.max(jnp.abs(g), axis=1, keepdims=True), 2.0**-100)
-        e = jnp.ceil(jnp.log2(top)) - 15.0
-        q = jnp.clip(jnp.round(g * jnp.exp2(-e)), -32767.0, 32767.0)
-        high, low = halves(q)
+        e = exponent(jnp.max(jnp.abs(g), axis=1, keepdims=True))
+        high, low = halves(quantize(g, e))
         rhs = jnp.concatenate([high, low, jnp.broadcast_to(e, (n, 128))], axis=1).astype(BF16)
         flat = flat_index(counts, W, iota((1, n), 1), cap)
         sel = jnp.where(flat == iota((W * cap, n), 0), 1.0, 0.0).astype(BF16)
@@ -405,7 +517,7 @@
 
     ucode, ue = encode(gu[...], ucnt, CAPU)
     msg[:, 0:CAPU, :] = ucode.astype(I16)
-    vcode, ve = encode(gv[...], icnt, CAPI)
+    vcode, ve = encode(0.5 * gv[...], icnt, CAPI)
     msg[:, CAPU : CAPU + CAPI, :] = vcode.astype(I16)
     wcode, we = encode(gw[...], wcnt, CAPX)
     shape = (W, CAPX, RANK)
@@ -423,15 +535,17 @@
 
     def ms_copy(s):
         return rcopy(
-            msg.at[wrap(me + s)],
+            msg.at[to(s)],
             mbuf.at[0, s],
             ms_ss.at[s],
             ms_rs.at[s],
-            {"wide": wrap(me + s)},
+            {"wide": to(s)},
         )
 
     peers(lambda s: ms_copy(s).start())
     mbuf[0, 0] = msg[me]
+    leave.append(lambda: peers(lambda s: ms_copy(s).wait_send()))
+    pend["ms"] = lambda: peers(lambda s: ms_copy(s).wait_recv())
 
     groups = W // GROUP
 
@@ -491,28 +605,20 @@
             high, low = halves(q.reshape(W * cap, RANK))
             acc[...] += dot(sel, jnp.concatenate([high, low], axis=1).astype(BF16))
 
-    for g in range(groups):
+    pend.pop("ms")
+    for g in GROUPS:
         for s in range(g * GROUP, (g + 1) * GROUP):
             if s > 0:
                 ms_copy(s).wait_recv()
         ring_copy(0, g).start()
         sib_copy(0, g).start()
+
     pr_hop(3)
-
-    def fa_wait(s):
-        rcopy(
-            fall.at[me],
-            fall.at[wrap(me - s)],
-            fa_ss.at[s],
-            fa_rs.at[s],
-            {"wide": wrap(me + s)},
-        ).wait_recv()
-
-    peers(fa_wait)
+    pend.pop("fa")()
     out_f[...] = fall[...].reshape(FD, RANK)
     add_rows(mbuf, 0)
     for h in range(1, NY):
-        for g in range(groups):
+        for g in GROUPS:
             ring_copy(h - 1, g).wait_recv()
             if h < NY - 1:
                 ring_copy(h, g).start()
@@ -525,28 +631,34 @@
         sib_copy(NY - 1, g).wait_recv()
     add_rows(sbuf, NY - 1)
 
-    out_u[...] = 256.0 * accu[:, 0:RANK] + accu[:, RANK:] + pring[NY - 2]
+    out_u[...] = 256.0 * accu[:, 0:RANK] + accu[:, RANK:] + gp[y]
     out_i[...] = 256.0 * acci[:, 0:RANK] + acci[:, RANK:]
     out_w[...] = 256.0 * accw[0:WS, 0:RANK] + accw[0:WS, RANK:]
 
-    def sent(s):
-        req_copy(s).wait_send()
-        row_copy(s).wait_send()
-        fr_copy(s).wait_send()
-        fa_copy(s).wait_send()
-        ms_copy(s).wait_send()
-
-    peers(sent)
-    f_copy.wait_send()
-    for q in range(NY):
-        x_copy(q).wait_send()
     for h in range(NY - 1):
-        pr_copy(h).wait_send()
         for g in range(groups):
             ring_copy(h, g).wait_send()
     for h in range(NY):
         for g in range(groups):
             sib_copy(h, g).wait_send()
+    for fn in pend.values():
+        fn()
+    for fn in leave:
+        fn()
+
+
+def finish(*refs):
+    n = (len(refs) - 1) // 3
+    src, dst, hold, sem = refs[:n], refs[n : 2 * n], refs[2 * n : 3 * n], refs[-1]
+    inward = [pltpu.make_async_copy(src[k], hold[k], sem.at[0, k]) for k in range(n)]
+    outward = [pltpu.make_async_copy(hold[k], dst[k], sem.at[1, k]) for k in range(n)]
+    for cp in inward:
+        cp.start()
+    for k in range(n):
+        inward[k].wait()
+        outward[k].start()
+    for cp in outward:
+        cp.wait()
 
 
 def local(
@@ -565,15 +677,6 @@
     week_counts,
     pos_cells,
 ):
-    lines = jnp.stack(
-        [
-            jnp.tile(user_req[0], (1, 128 // CAPU)),
-            jnp.tile(item_req[0], (1, 128 // CAPI)),
-            jnp.tile(jnp.pad(week_req[0], ((0, 0), (0, CAPX - CAPW))), (1, 128 // CAPX)),
-        ],
-        axis=1,
-    )
-    reqs = jnp.pad(lines, ((0, 0), (0, 5), (0, 0)))
     UR, IR, WR = user_table.shape[0], item_table.shape[0], week_table.shape[0]
     FD = feature_table.shape[0]
     US, IS, WS = UR // (2 * NY), IR // (2 * NY), WR // (2 * NY)
@@ -583,15 +686,16 @@
     anywhere = pl.BlockSpec(memory_space=pl.ANY)
     vmem = pl.BlockSpec(memory_space=pltpu.VMEM)
     smem = pl.BlockSpec(memory_space=pltpu.SMEM)
-    return pl.pallas_call(
+    shapes = (
+        jax.ShapeDtypeStruct((US, RANK), F32),
+        jax.ShapeDtypeStruct((IS, RANK), F32),
+        jax.ShapeDtypeStruct((WS, RANK), F32),
+        jax.ShapeDtypeStruct((FD, RANK), F32),
+    )
+    outs = pl.pallas_call(
         functools.partial(kernel, W, NY),
-        out_shape=(
-            jax.ShapeDtypeStruct((US, RANK), F32),
-            jax.ShapeDtypeStruct((IS, RANK), F32),
-            jax.ShapeDtypeStruct((WS, RANK), F32),
-            jax.ShapeDtypeStruct((FD, RANK), F32),
-        ),
-        in_specs=[anywhere] * 5 + [vmem] + [smem] * 3 + [vmem],
+        out_shape=shapes,
+        in_specs=[anywhere] * 5 + [vmem] * 3 + [smem] * 3 + [vmem],
         out_specs=(vmem, vmem, vmem, vmem),
         scratch_shapes=[
             V((UR, RANK), BF16),
@@ -602,11 +706,13 @@
             V((NY, US, FD), BF16),
             V((FD, RANK), BF16),
             V((W, 8, 128), I32),
+            V((W, 8, 128), I32),
             V((W // 2 * CAPU, UR), BF16),
             V((W, MSG, RANK), BF16),
             V((W, MSG, RANK), BF16),
             V((NY, US, RANK), F32),
-            V((NY - 1, US, RANK), F32),
+            V((NY - 1, US + 16, RANK), I16),
+            V((NY - 1, US + 16, RANK), I16),
             V((RANK, FD), F32),
             V((W, FC, RANK), F32),
             V((W, FC, RANK), F32),
@@ -614,7 +720,8 @@
             V((32, 128), I32),
             V((32, 8, 128), I32),
             V((1, pos_cells.shape[1]), F32),
-            V((2 * BU, BI), F32),
+            V((32, 128, 128), I32),
+            V((3 * BU, BI), F32),
             V((BU, BI), I32),
             V((BU, RANK), F32),
             V((32, RANK), F32),
@@ -623,6 +730,12 @@
             V((BU, RANK), F32),
             V((BI, RANK), F32),
             V((32, RANK), F32),
+            V((PAIR * BU, RANK), BF16),
+            V((PAIR * BU, RANK), BF16),
+            V((PAIR * BU, BI), F32),
+            V((PAIR * BU, BI), F32),
+            V((PAIR * BU, BI), BF16),
+            V((PAIR * BU, BI), BF16),
             V((W, MSG, RANK), I16),
             V((NY, W, MSG, RANK), I16),
             V((NY, W, MSG, RANK), I16),
@@ -658,13 +771,21 @@
         week_table,
         profile,
         feature_table,
-        reqs,
+        user_req[0],
+        item_req[0],
+        jnp.swapaxes(week_req[0], 0, 1),
         user_counts,
         item_counts,
         week_counts,
         pos_cells,
     )
-
+    return pl.pallas_call(
+        finish,
+        out_shape=shapes,
+        in_specs=[anywhere] * len(shapes),
+        out_specs=(anywhere,) * len(shapes),
+        scratch_shapes=[V(a.shape, a.dtype) for a in shapes] + [D((2, len(shapes)))],
+    )(*outs)
 
 def solution(mesh):
     W, NY = mesh.shape["wide"], mesh.shape["narrow"] // 2

time: 103 us -> 79.1 us (0.77)
  Pallas kernels: 91.8 us -> 78.1 us
  local copies, waits for them, and re-layouts: 9.79 us -> 0 us
    pallas_call x1 -> x2, Pallas kernels: 91.8 us -> 78.1 us  [the longest x1 76 us: local(): pl.pallas_call(functools.partial(kernel, W, NY), out_shape=shapes, in_spe...]
    unnamed x5 -> x0, local copies, waits for them, and re-layouts: 7.46 us -> none
    another operation x6 -> x0, local copies, waits for them, and re-layouts: 1.69 us -> none  [the longest x2 0.8 us: local(): jnp.tile(item_req[0], (1, 128 // CAPI))]
where the time goes in v2:
time: 79.1 us; the launch traced here: 78.9 us
  Pallas kernels  78.1 us (99%)
  between operations  0.8 us (1%)
    pallas_call x1, Pallas kernels, local(): pl.pallas_call(functools.partial(kernel, W, NY), out_shape=shapes, in_spe...  76 us
    pallas_call x1, Pallas kernels, local(): pl.pallas_call(finish, out_shape=shapes, in_specs=[anywhere] * len(shapes...  2.17 us

profile of v2, /device:TPU:1, one launch (start us, length us, event | category | flops | bytes accessed | tf_op | source)
XLA Modules:
  0.0 78.9 jit_solution(2897362139723685633)
XLA Ops:
  0.6 76.0 %shard_map.147 = (f32[512,256]{1,0:T(8,128)}, f32[256,256]{1,0:T(8,128)}, f32[8,256]{1,0:T(8,128)}, f32[512,256]{1,0:T(8,128)}) custom-call(bf16[4096,256]{1,0:T(8,128)(2,1)} %utab.1, bf16[2048,256]{1,0:T(8,128)(2,1)} %itab.1, bf16[64,256]{1,0:T(8,128)(2,1)} %wtab.1, bf16[4096,512]{1,0:T(8,128)(2,1)} %prof.1, bf16[512,256]{1,0:T(8,128)(2,1)} %ftab.1, ...), custom_call_target="tpu_custom_call" | custom-call | tf_op jit(solution)/shard_map/pallas_call | solution.py:695
  76.6 2.2 %shard_map.148 = (f32[512,256]{1,0:T(8,128)}, f32[256,256]{1,0:T(8,128)}, f32[8,256]{1,0:T(8,128)}, f32[512,256]{1,0:T(8,128)}) custom-call(f32[512,256]{1,0:T(8,128)} %get-tuple-element.8.refs_0_, f32[256,256]{1,0:T(8,128)} %get-tuple-element.9.refs_1_, f32[8,256]{1,0:T(8,128)} %get-tuple-element.10.refs_2_, f32[512,256]{1,0:T(8,128)} %get-tuple-element.11.refs_3_), custom_call_target="tpu_custom_call" | custom-call | tf_op jit(solution)/shard_map/pallas_call | solution.py:782

commit v3 on v2

--- a/solution.py
+++ b/solution.py
@@ -98,8 +98,10 @@
     rowsend,
     rowbuf,
     gp,
-    prsend,
-    pring,
+    pusend,
+    puring,
+    pisend,
+    piring,
     feat,
     fsend,
     frecv,
@@ -117,18 +119,25 @@
     gu,
     gv,
     gw,
-    uw0,
-    uw1,
+    uw,
+    gg,
     mm0,
     mm1,
-    gg0,
-    gg1,
-    msg,
-    mbuf,
-    sbuf,
-    accu,
-    acci,
-    accw,
+    umsg,
+    vmsg,
+    umine,
+    vmine,
+    utheirs,
+    vtheirs,
+    uid,
+    iid,
+    wid,
+    usc,
+    isc,
+    wsc,
+    urh,
+    irh,
+    wrh,
     load_sem,
     req_ss,
     req_rs,
@@ -140,14 +149,18 @@
     fr_rs,
     fa_ss,
     fa_rs,
-    pr_ss,
-    pr_rs,
-    ms_ss,
-    ms_rs,
-    ring_ss,
-    ring_rs,
-    sib_ss,
-    sib_rs,
+    pu_ss,
+    pu_rs,
+    pi_ss,
+    pi_rs,
+    mu_ss,
+    mu_rs,
+    mv_ss,
+    mv_rs,
+    su_ss,
+    su_rs,
+    sv_ss,
+    sv_rs,
 ):
     me = lax.axis_index("wide")
     nar = lax.axis_index("narrow")
@@ -377,28 +390,6 @@
 
     lax.fori_loop(0, NY, sib_rows, 0)
 
-    def pr_copy(h):
-        return rcopy(prsend.at[h], pring.at[h], pr_ss.at[h], pr_rs.at[h], {"narrow": nxt})
-
-    def pr_start(h, x):
-        e = exponent(jnp.max(jnp.abs(x), axis=0, keepdims=True))
-        prsend[h, 0:US, :] = quantize(x, e).astype(I32).astype(I16)
-        prsend[h, US:, :] = jnp.broadcast_to(e, (16, RANK)).astype(I32).astype(I16)
-        pr_copy(h).start()
-        leave.append(lambda: pr_copy(h).wait_send())
-        pend["pr"] = lambda: pr_copy(h).wait_recv()
-
-    def pr_hop(h):
-        pend.pop("pr")()
-        q = lax.rem(y - (h + 1) * step + 2 * NY, NY)
-        e = pring[h - 1, US:, :].astype(I32).astype(F32)[0:1, :]
-        x = pring[h - 1, 0:US, :].astype(I32).astype(F32) * jnp.exp2(e) + gp[q]
-        if h < NY - 1:
-            pr_start(h, x)
-        else:
-            gp[y] = x
-
-    pr_start(0, gp[lax.rem(y - step + NY, NY)])
 
     cacc[...] = jnp.zeros_like(cacc)
 
@@ -440,41 +431,49 @@
     gv[...] = jnp.zeros_like(gv)
     gw[...] = jnp.zeros_like(gw)
 
-    def lead(k, uw, mm):
-        for a in range(PAIR):
-            uw[BU * a : BU * (a + 1), :] = (uf[...] * wf[pl.ds(k + a, 1), :]).astype(BF16)
-        mm[...] = dot(uw[...], vt[...])
-
-    def work(k, uw, mm, gg):
-        place = jnp.where(k < FIELDS, 2 * k, jnp.where(k < 2 * FIELDS, 2 * (k - FIELDS) + 1, 2 * (k - FIELDS)))
+    def rows_of(k):
+        return pl.ds(pl.multiple_of(k * BU, BU), PAIR * BU)
+
+    def lead(k, mm):
+        mixed = [(uf[...] * wf[pl.ds(k + a, 1), :]).astype(BF16) for a in range(PAIR)]
+        mixed = jnp.concatenate(mixed, axis=0)
+        uw[rows_of(k), :] = mixed
+        mm[...] = dot(mixed, vt[...])
+
+    def work(k, mm):
+        place = jnp.where(
+            k < FIELDS,
+            2 * k,
+            jnp.where(k < 2 * FIELDS, 2 * (k - FIELDS) + 1, 2 * (k - FIELDS)),
+        )
         hits = bits[...] >> place
+        parts = []
         for a in range(PAIR):
             sign = jnp.where((hits & (1 << (2 * a))) != 0, -1.0, 1.0)
-            at = slice(BU * a, BU * (a + 1))
-            gg[at, :] = (jnp.tanh(mm[at, :]) + sign).astype(BF16)
-        q = dot(gg[...], vb[...])
+            parts.append((jnp.tanh(mm[BU * a : BU * (a + 1), :]) + sign).astype(BF16))
+        g = jnp.concatenate(parts, axis=0)
+        gg[rows_of(k), :] = g
+        q = dot(g, vb[...])
         total = gu[...]
         for a in range(PAIR):
             w, qa = wf[pl.ds(k + a, 1), :], q[BU * a : BU * (a + 1), :]
             total = total + qa * w
             gw[pl.ds(k + a, 1), :] = jnp.sum(qa * uf[...], axis=0, keepdims=True)
         gu[...] = total
-        gv[...] += dot_tn(gg[...], uw[...])
 
     def weeks(lo, hi):
         def both(n, z):
             k = 2 * PAIR * n
-            lead(k + PAIR, uw1, mm1)
-            work(k, uw0, mm0, gg0)
-            lead(k + 2 * PAIR, uw0, mm0)
-            work(k + PAIR, uw1, mm1, gg1)
+            lead(k + PAIR, mm1)
+            work(k, mm0)
+            lead(k + 2 * PAIR, mm0)
+            work(k + PAIR, mm1)
             return z
 
         lax.fori_loop(lo // (2 * PAIR), hi // (2 * PAIR), both, 0)
 
-    lead(0, uw0, mm0)
+    lead(0, mm0)
     weeks(0, 12)
-    pr_hop(1)
 
     pend.pop("fr")()
     total = frecv[0]
@@ -499,7 +498,6 @@
     leave.append(lambda: peers(lambda s: fa_copy(s).wait_send()))
     pend["fa"] = lambda: peers(fa_wait)
     weeks(12, BW)
-    pr_hop(2)
 
     def encode(g, counts, cap):
         n = g.shape[0]
@@ -515,10 +513,17 @@
         es = jnp.sum(es, axis=1, keepdims=True).astype(I32)
         return code.reshape(W, cap, RANK), es
 
+    def send_out(src, dst, ss, rs):
+        def copy(t):
+            return rcopy(src.at[to(t)], dst.at[t], ss.at[t], rs.at[t], {"wide": to(t)})
+
+        peers(lambda t: copy(t).start())
+        dst[0] = src[me]
+        leave.append(lambda: peers(lambda t: copy(t).wait_send()))
+        return copy
+
     ucode, ue = encode(gu[...], ucnt, CAPU)
-    msg[:, 0:CAPU, :] = ucode.astype(I16)
-    vcode, ve = encode(0.5 * gv[...], icnt, CAPI)
-    msg[:, CAPU : CAPU + CAPI, :] = vcode.astype(I16)
+    umsg[:, 0:CAPU, :] = ucode.astype(I16)
     wcode, we = encode(gw[...], wcnt, CAPX)
     shape = (W, CAPX, RANK)
     none = jnp.zeros_like(we)
@@ -526,54 +531,40 @@
     for r, left, right in (
         (8, reqs[:, 0:1, :], reqs[:, 1:2, :]),
         (9, reqs[:, 2:3, :], none),
-        (10, ue, ve),
+        (10, ue, none),
         (11, we, none),
     ):
         line = jnp.broadcast_to(jnp.concatenate([left, right], axis=2), shape)
         tail = jnp.where(iota(shape, 1) == r, line, tail)
-    msg[:, CAPU + CAPI : MSG, :] = tail.astype(I16)
-
-    def ms_copy(s):
-        return rcopy(
-            msg.at[to(s)],
-            mbuf.at[0, s],
-            ms_ss.at[s],
-            ms_rs.at[s],
-            {"wide": to(s)},
-        )
-
-    peers(lambda s: ms_copy(s).start())
-    mbuf[0, 0] = msg[me]
-    leave.append(lambda: peers(lambda s: ms_copy(s).wait_send()))
-    pend["ms"] = lambda: peers(lambda s: ms_copy(s).wait_recv())
+    umsg[:, CAPU:, :] = tail.astype(I16)
+    mu_copy = send_out(umsg, umine, mu_ss, mu_rs)
+
+    def value(n, z):
+        at = pl.ds(pl.multiple_of(n * 4 * BU, BU), 4 * BU)
+        gv[...] += dot_tn(gg[at, :], uw[at, :])
+        return z
+
+    lax.fori_loop(0, BW // 4, value, 0)
+    vcode, ve = encode(0.5 * gv[...], icnt, CAPI)
+    vmsg[:, 0:CAPI, :] = vcode.astype(I16)
+    line = jnp.concatenate([ve, none], axis=2)
+    vmsg[:, CAPI:, :] = jnp.broadcast_to(line, shape).astype(I16)
+    mv_copy = send_out(vmsg, vmine, mv_ss, mv_rs)
 
     groups = W // GROUP
 
-    def span(g):
-        return pl.ds(g * GROUP, GROUP)
-
-    def ring_copy(h, g):
-        return rcopy(
-            mbuf.at[h, span(g)],
-            mbuf.at[h + 1, span(g)],
-            ring_ss.at[h, g],
-            ring_rs.at[h, g],
-            {"narrow": nxt},
-        )
-
-    def sib_copy(h, g):
-        return rcopy(
-            mbuf.at[h, span(g)],
-            sbuf.at[h, span(g)],
-            sib_ss.at[h, g],
-            sib_rs.at[h, g],
-            {"narrow": sib},
-        )
-
-    share = nar
-    accu[...] = jnp.zeros_like(accu)
-    acci[...] = jnp.zeros_like(acci)
-    accw[...] = jnp.zeros_like(accw)
+    def share_out(copy, mine, theirs, ss, rs):
+        def sib_copy(g):
+            at = pl.ds(g * GROUP, GROUP)
+            return rcopy(mine.at[at], theirs.at[at], ss.at[g], rs.at[g], {"narrow": sib})
+
+        for g in GROUPS:
+            for t in range(g * GROUP, (g + 1) * GROUP):
+                if t > 0:
+                    copy(t).wait_recv()
+            sib_copy(g).start()
+            leave.append(lambda g=g: sib_copy(g).wait_send())
+        return lambda: [sib_copy(g).wait_recv() for g in GROUPS]
 
     def lanes(tail_rows, r, first, cap):
         each = 128 // cap
@@ -586,61 +577,107 @@
             pieces.append(piece)
         return jnp.concatenate(pieces, axis=1)
 
-    def add_rows(buf, h):
-        tail_rows = buf[h, :, CAPU + CAPI : MSG, :].astype(I32).astype(F32)
-        for acc, kind, lo, cap, size in (
-            (accu, 0, 0, CAPU, US),
-            (acci, 1, CAPU, CAPI, IS),
-            (accw, 2, CAPU + CAPI, CAPX, WS),
-        ):
-            r, first = (8, 128 * kind) if kind < 2 else (9, 0)
-            ids = lanes(tail_rows, r, first, cap)
-            scale = jnp.exp2(lanes(tail_rows, r + 2, first, cap))
-            rows = acc.shape[0]
-            place = (iota((rows, W * cap), 0) + share * size).astype(F32)
-            sel = jnp.where(ids == place, jnp.broadcast_to(scale, place.shape), 0.0).astype(BF16)
-            q = buf[h, :, lo : lo + cap, :].astype(I32).astype(F32)
-            if kind == 2:
-                q = jnp.where(iota(q.shape, 1) < CAPW, q, 0.0)
-            high, low = halves(q.reshape(W * cap, RANK))
-            acc[...] += dot(sel, jnp.concatenate([high, low], axis=1).astype(BF16))
-
-    pend.pop("ms")
-    for g in GROUPS:
-        for s in range(g * GROUP, (g + 1) * GROUP):
-            if s > 0:
-                ms_copy(s).wait_recv()
-        ring_copy(0, g).start()
-        sib_copy(0, g).start()
-
-    pr_hop(3)
+    def rows_in(buf, b, lo, cap, rhs):
+        n = W * cap
+        q = buf[:, lo : lo + cap, :].astype(I32).astype(F32)
+        if lo > 0:
+            q = jnp.where(iota(q.shape, 1) < CAPW, q, 0.0)
+        high, low = halves(q.reshape(n, RANK))
+        rhs[b * n : (b + 1) * n, 0:RANK] = high.astype(BF16)
+        rhs[b * n : (b + 1) * n, RANK:] = low.astype(BF16)
+
+    def unpack_u(buf, b):
+        tail_rows = buf[:, CAPU:, :].astype(I32).astype(F32)
+        nu, nw = slice(b * W * CAPU, (b + 1) * W * CAPU), slice(b * W * CAPX, (b + 1) * W * CAPX)
+        uid[:, nu] = lanes(tail_rows, 8, 0, CAPU)
+        iid[:, nu] = lanes(tail_rows, 8, 128, CAPI)
+        wid[:, nw] = lanes(tail_rows, 9, 0, CAPX)
+        usc[:, nu] = jnp.exp2(lanes(tail_rows, 10, 0, CAPU))
+        wsc[:, nw] = jnp.exp2(lanes(tail_rows, 11, 0, CAPX))
+        rows_in(buf, b, 0, CAPU, urh)
+        rows_in(buf, b, CAPU, CAPX, wrh)
+
+    def unpack_v(buf, b):
+        tail_rows = buf[:, CAPI:, :].astype(I32).astype(F32)
+        isc[:, b * W * CAPI : (b + 1) * W * CAPI] = jnp.exp2(lanes(tail_rows, 0, 0, CAPI))
+        rows_in(buf, b, 0, CAPI, irh)
+
+    def added(q, rows, size, ids, scale, rhs):
+        row = iota((rows, ids.shape[1]), 0)
+        place = row + (2 * q + c) * size
+        if rows > size:
+            place = jnp.where(row < size, place, -1)
+        place = place.astype(F32)
+        sel = jnp.where(ids[...] == place, jnp.broadcast_to(scale[...], place.shape), 0.0)
+        both = dot(sel.astype(BF16), rhs[...])
+        return 256.0 * both[:, 0:RANK] + both[:, RANK:]
+
+    def pu_copy(h):
+        return rcopy(pusend.at[h], puring.at[h], pu_ss.at[h], pu_rs.at[h], {"narrow": nxt})
+
+    def pi_copy(h):
+        return rcopy(pisend.at[h], piring.at[h], pi_ss.at[h], pi_rs.at[h], {"narrow": nxt})
+
+    def coded(x):
+        e = exponent(jnp.max(jnp.abs(x), axis=0, keepdims=True))
+        line = jnp.broadcast_to(e, (16, RANK)).astype(I32).astype(I16)
+        return quantize(x, e).astype(I32).astype(I16), line
+
+    def plain(code, line):
+        e = line.astype(I32).astype(F32)[0:1, :]
+        return code.astype(I32).astype(F32) * jnp.exp2(e)
+
+    def pu_start(h, x):
+        pusend[h, 0:US, :], pusend[h, US:, :] = coded(x)
+        pu_copy(h).start()
+        leave.append(lambda: pu_copy(h).wait_send())
+
+    def pi_start(h, x, w):
+        pisend[h, 0:IS, :], pisend[h, IS : IS + 16, :] = coded(x)
+        pisend[h, IS + 16 : IS + 32, :], pisend[h, IS + 32 :, :] = coded(w)
+        pi_copy(h).start()
+        leave.append(lambda: pi_copy(h).wait_send())
+
+    def at_hop(h):
+        return lax.rem(y - (h + 1) * step + 2 * NY, NY)
+
+    def users(h):
+        return added(at_hop(h), US, US, uid, usc, urh) + gp[at_hop(h)]
+
+    def items(h):
+        q = at_hop(h)
+        return added(q, IS, IS, iid, isc, irh), added(q, 16, WS, wid, wsc, wrh)
+
+    arrived = share_out(mu_copy, umine, utheirs, su_ss, su_rs)
+    unpack_u(umine, 0)
+    arrived()
+    unpack_u(utheirs, 1)
+    pu_start(0, users(0))
+    arrived = share_out(mv_copy, vmine, vtheirs, sv_ss, sv_rs)
+    unpack_v(vmine, 0)
+    arrived()
+    unpack_v(vtheirs, 1)
+    pi_start(0, *items(0))
     pend.pop("fa")()
     out_f[...] = fall[...].reshape(FD, RANK)
-    add_rows(mbuf, 0)
     for h in range(1, NY):
-        for g in GROUPS:
-            ring_copy(h - 1, g).wait_recv()
-            if h < NY - 1:
-                ring_copy(h, g).start()
-            sib_copy(h, g).start()
-        for g in range(groups):
-            sib_copy(h - 1, g).wait_recv()
-        add_rows(sbuf, h - 1)
-        add_rows(mbuf, h)
-    for g in range(groups):
-        sib_copy(NY - 1, g).wait_recv()
-    add_rows(sbuf, NY - 1)
-
-    out_u[...] = 256.0 * accu[:, 0:RANK] + accu[:, RANK:] + gp[y]
-    out_i[...] = 256.0 * acci[:, 0:RANK] + acci[:, RANK:]
-    out_w[...] = 256.0 * accw[0:WS, 0:RANK] + accw[0:WS, RANK:]
-
-    for h in range(NY - 1):
-        for g in range(groups):
-            ring_copy(h, g).wait_send()
-    for h in range(NY):
-        for g in range(groups):
-            sib_copy(h, g).wait_send()
+        xu = users(h)
+        pu_copy(h - 1).wait_recv()
+        xu += plain(puring[h - 1, 0:US, :], puring[h - 1, US:, :])
+        if h < NY - 1:
+            pu_start(h, xu)
+        else:
+            out_u[...] = xu
+        xi, xw = items(h)
+        pi_copy(h - 1).wait_recv()
+        xi += plain(piring[h - 1, 0:IS, :], piring[h - 1, IS : IS + 16, :])
+        xw += plain(piring[h - 1, IS + 16 : IS + 32, :], piring[h - 1, IS + 32 :, :])
+        if h < NY - 1:
+            pi_start(h, xi, xw)
+        else:
+            out_i[...] = xi
+            out_w[...] = xw[0:WS, :]
+
     for fn in pend.values():
         fn()
     for fn in leave:
@@ -713,6 +750,8 @@
             V((NY, US, RANK), F32),
             V((NY - 1, US + 16, RANK), I16),
             V((NY - 1, US + 16, RANK), I16),
+            V((NY - 1, IS + 48, RANK), I16),
+            V((NY - 1, IS + 48, RANK), I16),
             V((RANK, FD), F32),
             V((W, FC, RANK), F32),
             V((W, FC, RANK), F32),
@@ -730,18 +769,25 @@
             V((BU, RANK), F32),
             V((BI, RANK), F32),
             V((32, RANK), F32),
-            V((PAIR * BU, RANK), BF16),
-            V((PAIR * BU, RANK), BF16),
+            V(((BW + PAIR) * BU, RANK), BF16),
+            V((BW * BU, BI), BF16),
             V((PAIR * BU, BI), F32),
             V((PAIR * BU, BI), F32),
-            V((PAIR * BU, BI), BF16),
-            V((PAIR * BU, BI), BF16),
-            V((W, MSG, RANK), I16),
-            V((NY, W, MSG, RANK), I16),
-            V((NY, W, MSG, RANK), I16),
-            V((US, 2 * RANK), F32),
-            V((IS, 2 * RANK), F32),
-            V((16, 2 * RANK), F32),
+            V((W, CAPU + CAPX, RANK), I16),
+            V((W, CAPI + CAPX, RANK), I16),
+            V((W, CAPU + CAPX, RANK), I16),
+            V((W, CAPI + CAPX, RANK), I16),
+            V((W, CAPU + CAPX, RANK), I16),
+            V((W, CAPI + CAPX, RANK), I16),
+            V((1, 2 * W * CAPU), F32),
+            V((1, 2 * W * CAPI), F32),
+            V((1, 2 * W * CAPX), F32),
+            V((1, 2 * W * CAPU), F32),
+            V((1, 2 * W * CAPI), F32),
+            V((1, 2 * W * CAPX), F32),
+            V((2 * W * CAPU, 2 * RANK), BF16),
+            V((2 * W * CAPI, 2 * RANK), BF16),
+            V((2 * W * CAPX, 2 * RANK), BF16),
             D((5,)),
             D((W,)),
             D((W,)),
@@ -755,12 +801,16 @@
             D((W,)),
             D((NY - 1,)),
             D((NY - 1,)),
-            D((W,)),
-            D((W,)),
-            D((NY - 1, groups)),
-            D((NY - 1, groups)),
-            D((NY, groups)),
-            D((NY, groups)),
+            D((NY - 1,)),
+            D((NY - 1,)),
+            D((W,)),
+            D((W,)),
+            D((W,)),
+            D((W,)),
+            D((groups,)),
+            D((groups,)),
+            D((groups,)),
+            D((groups,)),
         ],
         compiler_params=pltpu.CompilerParams(
             collective_id=0, has_side_effects=True, vmem_limit_bytes=56 << 20

time: 79.1 us -> 73 us (0.923)
  Pallas kernels: 78.1 us -> 72 us
    pallas_call x1, Pallas kernels: 76 us -> 69.8 us  [local(): pl.pallas_call(functools.partial(kernel, W, NY), out_shape=shapes, in_spe...]
where the time goes in v3:
time: 73 us; the launch traced here: 72.8 us
  Pallas kernels  72 us (99%)
  between operations  0.8 us (1%)
    pallas_call x1, Pallas kernels, local(): pl.pallas_call(functools.partial(kernel, W, NY), out_shape=shapes, in_spe...  69.8 us
    pallas_call x1, Pallas kernels, local(): pl.pallas_call(finish, out_shape=shapes, in_specs=[anywhere] * len(shapes...  2.17 us

profile of v3, /device:TPU:1, one launch (start us, length us, event | category | flops | bytes accessed | tf_op | source)
XLA Modules:
  0.0 72.8 jit_solution(10136440058961856082)
XLA Ops:
  0.6 69.8 %shard_map.147 = (f32[512,256]{1,0:T(8,128)}, f32[256,256]{1,0:T(8,128)}, f32[8,256]{1,0:T(8,128)}, f32[512,256]{1,0:T(8,128)}) custom-call(bf16[4096,256]{1,0:T(8,128)(2,1)} %utab.1, bf16[2048,256]{1,0:T(8,128)(2,1)} %itab.1, bf16[64,256]{1,0:T(8,128)(2,1)} %wtab.1, bf16[4096,512]{1,0:T(8,128)(2,1)} %prof.1, bf16[512,256]{1,0:T(8,128)(2,1)} %ftab.1, ...), custom_call_target="tpu_custom_call" | custom-call | tf_op jit(solution)/shard_map/pallas_call | solution.py:732
  70.5 2.2 %shard_map.148 = (f32[512,256]{1,0:T(8,128)}, f32[256,256]{1,0:T(8,128)}, f32[8,256]{1,0:T(8,128)}, f32[512,256]{1,0:T(8,128)}) custom-call(f32[512,256]{1,0:T(8,128)} %get-tuple-element.8.refs_0_, f32[256,256]{1,0:T(8,128)} %get-tuple-element.9.refs_1_, f32[8,256]{1,0:T(8,128)} %get-tuple-element.10.refs_2_, f32[512,256]{1,0:T(8,128)} %get-tuple-element.11.refs_3_), custom_call_target="tpu_custom_call" | custom-call | tf_op jit(solution)/shard_map/pallas_call | solution.py:832

commit v4 on v3

--- a/solution.py
+++ b/solution.py
@@ -377,19 +377,6 @@
             {"wide": to(s)},
         )
 
-    peers(lambda s: fr_copy(s).start())
-    frecv[0] = fsend[me]
-    leave.append(lambda: peers(lambda s: fr_copy(s).wait_send()))
-    pend["fr"] = lambda: peers(lambda s: fr_copy(s).wait_recv())
-    pend.pop("x")()
-
-    def sib_rows(q, z):
-        row = pl.multiple_of((2 * q + c) * US, US)
-        gp[q] += 0.0625 * dot(resid(row, x2[q], f2[...]), f2[...])
-        return z
-
-    lax.fori_loop(0, NY, sib_rows, 0)
-
 
     cacc[...] = jnp.zeros_like(cacc)
 
@@ -422,6 +409,10 @@
     pu, pv, pw = pick(ucnt, BU, CAPU), pick(icnt, BI, CAPI), pick(wcnt, 32, CAPX)
 
     pend.pop("row")()
+    peers(lambda s: fr_copy(s).start())
+    frecv[0] = fsend[me]
+    leave.append(lambda: peers(lambda s: fr_copy(s).wait_send()))
+    pend["fr"] = lambda: peers(lambda s: fr_copy(s).wait_recv())
     uf[...] = dot(pu, rowbuf[:, 0:CAPU, :].reshape(W * CAPU, RANK))
     vf = dot(pv, rowbuf[:, CAPU : CAPU + CAPI, :].reshape(W * CAPI, RANK))
     wf[...] = dot(pw, rowbuf[:, CAPU + CAPI : MSG, :].reshape(W * CAPX, RANK))
@@ -473,31 +464,7 @@
         lax.fori_loop(lo // (2 * PAIR), hi // (2 * PAIR), both, 0)
 
     lead(0, mm0)
-    weeks(0, 12)
-
-    pend.pop("fr")()
-    total = frecv[0]
-    for s in range(1, W):
-        total = total + frecv[s]
-    fall[me] = total
-
-    def fa_copy(s):
-        return rcopy(fall.at[me], fall.at[me], fa_ss.at[s], fa_rs.at[s], {"wide": to(s)})
-
-    peers(lambda s: fa_copy(s).start())
-
-    def fa_wait(s):
-        rcopy(
-            fall.at[me],
-            fall.at[frm(s)],
-            fa_ss.at[s],
-            fa_rs.at[s],
-            {"wide": to(s)},
-        ).wait_recv()
-
-    leave.append(lambda: peers(lambda s: fa_copy(s).wait_send()))
-    pend["fa"] = lambda: peers(fa_wait)
-    weeks(12, BW)
+    weeks(0, BW)
 
     def encode(g, counts, cap):
         n = g.shape[0]
@@ -551,6 +518,39 @@
     vmsg[:, CAPI:, :] = jnp.broadcast_to(line, shape).astype(I16)
     mv_copy = send_out(vmsg, vmine, mv_ss, mv_rs)
 
+    pend.pop("x")()
+
+    def sib_rows(q, z):
+        row = pl.multiple_of((2 * q + c) * US, US)
+        gp[q] += 0.0625 * dot(resid(row, x2[q], f2[...]), f2[...])
+        return z
+
+    lax.fori_loop(0, NY, sib_rows, 0)
+
+
+    pend.pop("fr")()
+    total = frecv[0]
+    for s in range(1, W):
+        total = total + frecv[s]
+    fall[me] = total
+
+    def fa_copy(s):
+        return rcopy(fall.at[me], fall.at[me], fa_ss.at[s], fa_rs.at[s], {"wide": to(s)})
+
+    peers(lambda s: fa_copy(s).start())
+
+    def fa_wait(s):
+        rcopy(
+            fall.at[me],
+            fall.at[frm(s)],
+            fa_ss.at[s],
+            fa_rs.at[s],
+            {"wide": to(s)},
+        ).wait_recv()
+
+    leave.append(lambda: peers(lambda s: fa_copy(s).wait_send()))
+    pend["fa"] = lambda: peers(fa_wait)
+
     groups = W // GROUP
 
     def share_out(copy, mine, theirs, ss, rs):
@@ -658,10 +658,11 @@
     arrived()
     unpack_v(vtheirs, 1)
     pi_start(0, *items(0))
-    pend.pop("fa")()
-    out_f[...] = fall[...].reshape(FD, RANK)
     for h in range(1, NY):
         xu = users(h)
+        if h == NY - 1:
+            pend.pop("fa")()
+            out_f[...] = fall[...].reshape(FD, RANK)
         pu_copy(h - 1).wait_recv()
         xu += plain(puring[h - 1, 0:US, :], puring[h - 1, US:, :])
         if h < NY - 1:

time: 73 us -> 66.9 us (0.916)
  Pallas kernels: 72 us -> 65.9 us
    pallas_call x1, Pallas kernels: 69.8 us -> 63.7 us  [local(): pl.pallas_call(functools.partial(kernel, W, NY), out_shape=shapes, in_spe...]
where the time goes in v4:
time: 66.9 us; the launch traced here: 66.7 us
  Pallas kernels  65.9 us (99%)
  between operations  0.8 us (1%)
    pallas_call x1, Pallas kernels, local(): pl.pallas_call(functools.partial(kernel, W, NY), out_shape=shapes, in_spe...  63.7 us
    pallas_call x1, Pallas kernels, local(): pl.pallas_call(finish, out_shape=shapes, in_specs=[anywhere] * len(shapes...  2.17 us

profile of v4, /device:TPU:1, one launch (start us, length us, event | category | flops | bytes accessed | tf_op | source)
XLA Modules:
  0.0 66.7 jit_solution(1776559479156705411)
XLA Ops:
  0.6 63.7 %shard_map.147 = (f32[512,256]{1,0:T(8,128)}, f32[256,256]{1,0:T(8,128)}, f32[8,256]{1,0:T(8,128)}, f32[512,256]{1,0:T(8,128)}) custom-call(bf16[4096,256]{1,0:T(8,128)(2,1)} %utab.1, bf16[2048,256]{1,0:T(8,128)(2,1)} %itab.1, bf16[64,256]{1,0:T(8,128)(2,1)} %wtab.1, bf16[4096,512]{1,0:T(8,128)(2,1)} %prof.1, bf16[512,256]{1,0:T(8,128)(2,1)} %ftab.1, ...), custom_call_target="tpu_custom_call" | custom-call | tf_op jit(solution)/shard_map/pallas_call | solution.py:733
  64.3 2.2 %shard_map.148 = (f32[512,256]{1,0:T(8,128)}, f32[256,256]{1,0:T(8,128)}, f32[8,256]{1,0:T(8,128)}, f32[512,256]{1,0:T(8,128)}) custom-call(f32[512,256]{1,0:T(8,128)} %get-tuple-element.8.refs_0_, f32[256,256]{1,0:T(8,128)} %get-tuple-element.9.refs_1_, f32[8,256]{1,0:T(8,128)} %get-tuple-element.10.refs_2_, f32[512,256]{1,0:T(8,128)} %get-tuple-element.11.refs_3_), custom_call_target="tpu_custom_call" | custom-call | tf_op jit(solution)/shard_map/pallas_call | solution.py:833

commit v5 on v4

--- a/solution.py
+++ b/solution.py
@@ -227,46 +227,6 @@
     for o in range(W):
         reqs[o, 2:3, :] = used[o : o + 1, :]
         reqs[o, 3:8, :] = jnp.zeros((5, 128), I32)
-    pl.semaphore_wait(barrier, W - 1 + 3)
-
-    def req_copy(s):
-        return rcopy(
-            reqs.at[to(s)],
-            rq.at[s],
-            req_ss.at[s],
-            req_rs.at[s],
-            {"wide": to(s)},
-        )
-
-    peers(lambda s: req_copy(s).start())
-    rq[0] = reqs[me]
-    leave.append(lambda: peers(lambda s: req_copy(s).wait_send()))
-    pend["rq"] = lambda: peers(lambda s: req_copy(s).wait_recv())
-
-    def x_copy(q):
-        row = pl.multiple_of((2 * q + 1 - c) * US, US)
-        return rcopy(
-            prof.at[pl.ds(row, US), :], x2.at[q], x_ss.at[q], x_rs.at[q], {"narrow": sib}
-        )
-
-    f_copy = rcopy(ftab, f2, x_ss.at[NY], x_rs.at[NY], {"narrow": sib})
-    f_copy.start()
-    for q in range(NY):
-        x_copy(q).start()
-
-    def x_wait():
-        f_copy.wait_recv()
-        for q in range(NY):
-            x_copy(q).wait_recv()
-
-    def x_sent():
-        f_copy.wait_send()
-        for q in range(NY):
-            x_copy(q).wait_send()
-
-    pend["x"] = x_wait
-    leave.append(x_sent)
-
     big = 1 << 30
 
     def least(xs):
@@ -283,6 +243,46 @@
     )
     for k in range(lines):
         spread[k] = jnp.broadcast_to(pt[:, k : k + 1], (128, 128))
+
+    pl.semaphore_wait(barrier, W - 1 + 3)
+
+    def req_copy(s):
+        return rcopy(
+            reqs.at[to(s)],
+            rq.at[s],
+            req_ss.at[s],
+            req_rs.at[s],
+            {"wide": to(s)},
+        )
+
+    peers(lambda s: req_copy(s).start())
+    rq[0] = reqs[me]
+    leave.append(lambda: peers(lambda s: req_copy(s).wait_send()))
+    pend["rq"] = lambda: peers(lambda s: req_copy(s).wait_recv())
+
+    def x_copy(q):
+        row = pl.multiple_of((2 * q + 1 - c) * US, US)
+        return rcopy(
+            prof.at[pl.ds(row, US), :], x2.at[q], x_ss.at[q], x_rs.at[q], {"narrow": sib}
+        )
+
+    f_copy = rcopy(ftab, f2, x_ss.at[NY], x_rs.at[NY], {"narrow": sib})
+    f_copy.start()
+    for q in range(NY):
+        x_copy(q).start()
+
+    def x_wait():
+        f_copy.wait_recv()
+        for q in range(NY):
+            x_copy(q).wait_recv()
+
+    def x_sent():
+        f_copy.wait_send()
+        for q in range(NY):
+            x_copy(q).wait_send()
+
+    pend["x"] = x_wait
+    leave.append(x_sent)
 
     def compare(k, block, masked):
         for a in range(BLOCK):

time: 66.9 us -> 66.2 us (0.990)
  Pallas kernels: 65.9 us -> 65.2 us
where the time goes in v5:
time: 66.2 us; the launch traced here: 66 us
  Pallas kernels  65.2 us (98%)
  between operations  0.8 us (1%)
    pallas_call x1, Pallas kernels, local(): pl.pallas_call(functools.partial(kernel, W, NY), out_shape=shapes, in_spe...  63.1 us
    pallas_call x1, Pallas kernels, local(): pl.pallas_call(finish, out_shape=shapes, in_specs=[anywhere] * len(shapes...  2.17 us

profile of v5, /device:TPU:1, one launch (start us, length us, event | category | flops | bytes accessed | tf_op | source)
XLA Modules:
  0.0 66.0 jit_solution(3648843855151640125)
XLA Ops:
  0.6 63.1 %shard_map.147 = (f32[512,256]{1,0:T(8,128)}, f32[256,256]{1,0:T(8,128)}, f32[8,256]{1,0:T(8,128)}, f32[512,256]{1,0:T(8,128)}) custom-call(bf16[4096,256]{1,0:T(8,128)(2,1)} %utab.1, bf16[2048,256]{1,0:T(8,128)(2,1)} %itab.1, bf16[64,256]{1,0:T(8,128)(2,1)} %wtab.1, bf16[4096,512]{1,0:T(8,128)(2,1)} %prof.1, bf16[512,256]{1,0:T(8,128)(2,1)} %ftab.1, ...), custom_call_target="tpu_custom_call" | custom-call | tf_op jit(solution)/shard_map/pallas_call | solution.py:733
  63.7 2.2 %shard_map.148 = (f32[512,256]{1,0:T(8,128)}, f32[256,256]{1,0:T(8,128)}, f32[8,256]{1,0:T(8,128)}, f32[512,256]{1,0:T(8,128)}) custom-call(f32[512,256]{1,0:T(8,128)} %get-tuple-element.8.refs_0_, f32[256,256]{1,0:T(8,128)} %get-tuple-element.9.refs_1_, f32[8,256]{1,0:T(8,128)} %get-tuple-element.10.refs_2_, f32[512,256]{1,0:T(8,128)} %get-tuple-element.11.refs_3_), custom_call_target="tpu_custom_call" | custom-call | tf_op jit(solution)/shard_map/pallas_call | solution.py:833

commit v6 on v5

--- a/solution.py
+++ b/solution.py
@@ -528,29 +528,6 @@
     lax.fori_loop(0, NY, sib_rows, 0)
 
 
-    pend.pop("fr")()
-    total = frecv[0]
-    for s in range(1, W):
-        total = total + frecv[s]
-    fall[me] = total
-
-    def fa_copy(s):
-        return rcopy(fall.at[me], fall.at[me], fa_ss.at[s], fa_rs.at[s], {"wide": to(s)})
-
-    peers(lambda s: fa_copy(s).start())
-
-    def fa_wait(s):
-        rcopy(
-            fall.at[me],
-            fall.at[frm(s)],
-            fa_ss.at[s],
-            fa_rs.at[s],
-            {"wide": to(s)},
-        ).wait_recv()
-
-    leave.append(lambda: peers(lambda s: fa_copy(s).wait_send()))
-    pend["fa"] = lambda: peers(fa_wait)
-
     groups = W // GROUP
 
     def share_out(copy, mine, theirs, ss, rs):
@@ -653,6 +630,29 @@
     arrived()
     unpack_u(utheirs, 1)
     pu_start(0, users(0))
+
+    pend.pop("fr")()
+    total = frecv[0]
+    for s in range(1, W):
+        total = total + frecv[s]
+    fall[me] = total
+
+    def fa_copy(s):
+        return rcopy(fall.at[me], fall.at[me], fa_ss.at[s], fa_rs.at[s], {"wide": to(s)})
+
+    peers(lambda s: fa_copy(s).start())
+
+    def fa_wait(s):
+        rcopy(
+            fall.at[me],
+            fall.at[frm(s)],
+            fa_ss.at[s],
+            fa_rs.at[s],
+            {"wide": to(s)},
+        ).wait_recv()
+
+    leave.append(lambda: peers(lambda s: fa_copy(s).wait_send()))
+    pend["fa"] = lambda: peers(fa_wait)
     arrived = share_out(mv_copy, vmine, vtheirs, sv_ss, sv_rs)
     unpack_v(vmine, 0)
     arrived()

time: 66.2 us -> 66.1 us (level)
  no operation moved by 1% of the time
where the time goes in v6:
time: 66.1 us; the launch traced here: 65.9 us
  Pallas kernels  65.1 us (98%)
  between operations  0.8 us (1%)
    pallas_call x1, Pallas kernels, local(): pl.pallas_call(functools.partial(kernel, W, NY), out_shape=shapes, in_spe...  62.9 us
    pallas_call x1, Pallas kernels, local(): pl.pallas_call(finish, out_shape=shapes, in_specs=[anywhere] * len(shapes...  2.17 us

profile of v6, /device:TPU:1, one launch (start us, length us, event | category | flops | bytes accessed | tf_op | source)
XLA Modules:
  0.0 65.9 jit_solution(9660873626851479819)
XLA Ops:
  0.6 62.9 %shard_map.147 = (f32[512,256]{1,0:T(8,128)}, f32[256,256]{1,0:T(8,128)}, f32[8,256]{1,0:T(8,128)}, f32[512,256]{1,0:T(8,128)}) custom-call(bf16[4096,256]{1,0:T(8,128)(2,1)} %utab.1, bf16[2048,256]{1,0:T(8,128)(2,1)} %itab.1, bf16[64,256]{1,0:T(8,128)(2,1)} %wtab.1, bf16[4096,512]{1,0:T(8,128)(2,1)} %prof.1, bf16[512,256]{1,0:T(8,128)(2,1)} %ftab.1, ...), custom_call_target="tpu_custom_call" | custom-call | tf_op jit(solution)/shard_map/pallas_call | solution.py:733
  63.6 2.2 %shard_map.148 = (f32[512,256]{1,0:T(8,128)}, f32[256,256]{1,0:T(8,128)}, f32[8,256]{1,0:T(8,128)}, f32[512,256]{1,0:T(8,128)}) custom-call(f32[512,256]{1,0:T(8,128)} %get-tuple-element.8.refs_0_, f32[256,256]{1,0:T(8,128)} %get-tuple-element.9.refs_1_, f32[8,256]{1,0:T(8,128)} %get-tuple-element.10.refs_2_, f32[512,256]{1,0:T(8,128)} %get-tuple-element.11.refs_3_), custom_call_target="tpu_custom_call" | custom-call | tf_op jit(solution)/shard_map/pallas_call | solution.py:833
